TPU v7x, 128 devices: a whole 4x4x4 slice. The times are simulated.
128 devices in a mesh: bx: 8 (over y_lo, z), by: 16 (over x, y_hi, core).
Axes of the slice: x: 4, y: 4 (y_hi: 2, y_lo: 2; y = y_hi * 2 + y_lo), z: 4, core: 2. Of those that a mesh axis runs over, the one named last changes fastest.
Arguments:
- positions: float32 [3, 16384], P(None, ('bx', 'by')), may hold values from 0 to 16, as said below
- tangent: float32 [3, 16384], P(None, ('bx', 'by')), may hold values from -6 to 6
- embedding: float32 [16384, 256], P(('bx', 'by')), may hold values from -6 to 6
- counts: int32 [128], P(('bx', 'by')), may hold values from 64 to 128, as said below
- neighbours: int32 [32, 16384], P(None, ('bx', 'by')), may hold values from 0 to 191, as said below
- send_rows: int32 [128, 64], P(('bx', 'by')), may hold values from 0 to 127
- w_one_in: float32 [256, 256], replicated, may hold values from -0.375 to 0.375
- w_one_out: float32 [256, 512], replicated, may hold values from -0.375 to 0.375
- filter_one: float32 [20, 512], replicated, may hold values from -0.3125 to 0.3125
- w_left: float32 [256, 256], replicated, may hold values from -0.375 to 0.375
- w_right: float32 [256, 256], replicated, may hold values from -0.375 to 0.375
- w_two_in: float32 [256, 256], replicated, may hold values from -0.375 to 0.375
- w_two_out: float32 [256, 256], replicated, may hold values from -0.375 to 0.375
- filter_two: float32 [20, 256], replicated, may hold values from -0.3125 to 0.3125
- w_hidden: float32 [256, 256], replicated, may hold values from -0.375 to 0.375
- w_energy: float32 [256], replicated, may hold values from -0.375 to 0.375
Outputs:
- forces: float32 [3, 16384], P(None, ('bx', 'by'))
- hessian_tangent: float32 [3, 16384], P(None, ('bx', 'by'))
Inputs may be any that keep to these rules, and one draw needn't show every extreme that they name: The live atoms of a brick are its first counts rows; every count is a multiple of 32; some brick holds 128 live atoms and some 128 // 2. `neighbours`: the 32 slots of an atom are distinct; each is a live row of its own brick other than the atom's own row, or a slot of a neighbouring brick that exists in the sheet. `positions`: atom n lies within one unit of its brick's indices along x and y, with the third coordinate in [0, 0.3).
All inputs are finite; a program needn't handle non-finite values.
Results may differ from a plain program's by a relative error of at most 0.0003.
Values sent between devices are 32-bit elements; how exact they have to be, the bound alone decides.
A program may use at most 192 MiB of HBM per device.

v0:
```python
import math

import jax
import jax.numpy as jnp
from jax import lax
from jax.sharding import PartitionSpec as P

highest = lax.Precision.HIGHEST
cutoff_radius = 3.0
softening = 0.01
offsets = ((-1, -1), (-1, 0), (-1, 1), (0, -1), (0, 1), (1, -1), (1, 0), (1, 1))


def passed_along(block, axis, distance):
    devices = range(lax.axis_size(axis))
    route = [(i - distance, i) for i in devices if i - distance in devices]
    return lax.ppermute(block, axis, route)


def project_rows(features, w_inner, w_outer):
    inner = jax.nn.silu(jnp.dot(features, w_inner, precision=highest))
    return jnp.dot(inner, w_outer, precision=highest)


def geometry(pos_table, own_lists, basis_count):
    own_rows = own_lists.shape[1]
    centre = pos_table[:, :own_rows]
    others = jnp.take(pos_table, own_lists, axis=1)
    offset = others - centre[:, None, :]
    distance = jnp.sqrt(jnp.sum(offset * offset, axis=0) + softening)
    direction = offset / distance[None]
    orders = jnp.arange(1, basis_count + 1).astype(distance.dtype)
    radial = (
        jnp.sin(orders[:, None, None] * (math.pi / cutoff_radius) * distance[None]) / distance[None]
    )
    envelope = 0.5 * (jnp.cos(math.pi / cutoff_radius * distance) + 1.0)
    return (radial, envelope, direction)


def edge_weights(radial, envelope, filter_table):
    mixed = jnp.einsum("qkr,qc->krc", radial, filter_table, precision=highest)
    return mixed * envelope[:, :, None]


def first_layer(pos_table, phi_table, embed_own, own_lists, filter_one, w_left, w_right):
    radial, envelope, direction = geometry(pos_table, own_lists, filter_one.shape[0])
    scale_edges = 1.0 / math.sqrt(own_lists.shape[0])
    message = jnp.take(phi_table, own_lists, axis=0) * edge_weights(radial, envelope, filter_one)
    channels = embed_own.shape[1]
    scalar_part = scale_edges * jnp.sum(message[:, :, :channels], axis=0)
    vector_part = scale_edges * jnp.einsum(
        "ckr,krf->crf", direction, message[:, :, channels:], precision=highest
    )
    left_map = jnp.einsum("crf,fg->crg", vector_part, w_left, precision=highest)
    right_map = jnp.einsum("crf,fg->crg", vector_part, w_right, precision=highest)
    return embed_own + scalar_part + jnp.sum(left_map * right_map, axis=0)


def second_layer(
    pos_table, phi_table, state_own, own_lists, live_rows, filter_two, w_hidden, w_energy
):
    geometry_parts = geometry(pos_table, own_lists, filter_two.shape[0])
    scale_edges = 1.0 / math.sqrt(own_lists.shape[0])
    weighted = jnp.take(phi_table, own_lists, axis=0) * edge_weights(
        geometry_parts[0], geometry_parts[1], filter_two
    )
    message = scale_edges * jnp.sum(weighted, axis=0)
    hidden_rows = jax.nn.silu(jnp.dot(state_own + message, w_hidden, precision=highest))
    return jnp.sum(live_rows * jnp.dot(hidden_rows, w_energy, precision=highest))


def move_bx(payload, stride):
    return passed_along(payload, "bx", stride)


def move_by(payload, stride):
    return passed_along(payload, "by", stride)


def back_bx(payload, stride):
    return passed_along(payload, "bx", stride)


def back_by(payload, stride):
    return passed_along(payload, "by", stride)


def place_at(along_first, along_second):
    return (along_first, along_second)


def joined(portions, members):
    return tuple(
        (jnp.concatenate([portion[column] for portion in portions], 0) for column in range(members))
    )


def take_block(arrived, number, ghost_count):
    return tuple((member[number * ghost_count : (number + 1) * ghost_count] for member in arrived))


def spread(payload, send_index, moves):
    ghost_count = send_index.shape[0] // 8
    members = len(payload)

    def toward(target):
        number = offsets.index(target)
        chosen = send_index[number * ghost_count : (number + 1) * ghost_count]
        return tuple((jnp.take(member, chosen, axis=0) for member in payload))

    by_slot = {}
    carried = {}
    for heading in (1, -1):
        portions = [toward(place_at(heading, across)) for across in (-1, 0, 1)]
        arrived = moves[0](joined(portions, members), heading)
        by_slot[place_at(-heading, 0)] = take_block(arrived, 1, ghost_count)
        carried[heading, -1] = take_block(arrived, 0, ghost_count)
        carried[heading, 1] = take_block(arrived, 2, ghost_count)
    for across in (1, -1):
        portions = [toward(place_at(0, across)), carried[1, across], carried[-1, across]]
        arrived = moves[1](joined(portions, members), across)
        by_slot[place_at(0, -across)] = take_block(arrived, 0, ghost_count)
        by_slot[place_at(-1, -across)] = take_block(arrived, 1, ghost_count)
        by_slot[place_at(1, -across)] = take_block(arrived, 2, ghost_count)
    return tuple(
        (
            jnp.concatenate([by_slot[target][column] for target in offsets], 0)
            for column in range(members)
        )
    )


def gather_back(payload, send_index, own_rows, moves):
    ghost_count = send_index.shape[0] // 8
    members = len(payload)

    def from_slot(target):
        number = offsets.index(target)
        return tuple(
            (member[number * ghost_count : (number + 1) * ghost_count] for member in payload)
        )

    toward_cot = {}
    carried = {}
    for across in (1, -1):
        portions = [
            from_slot(place_at(0, -across)),
            from_slot(place_at(-1, -across)),
            from_slot(place_at(1, -across)),
        ]
        arrived = moves[1](joined(portions, members), -across)
        toward_cot[place_at(0, across)] = take_block(arrived, 0, ghost_count)
        carried[1, across] = take_block(arrived, 1, ghost_count)
        carried[-1, across] = take_block(arrived, 2, ghost_count)
    for heading in (1, -1):
        portions = [carried[heading, -1], from_slot(place_at(-heading, 0)), carried[heading, 1]]
        arrived = moves[0](joined(portions, members), -heading)
        toward_cot[place_at(heading, -1)] = take_block(arrived, 0, ghost_count)
        toward_cot[place_at(heading, 0)] = take_block(arrived, 1, ghost_count)
        toward_cot[place_at(heading, 1)] = take_block(arrived, 2, ghost_count)
    summed = []
    for column in range(members):
        values = jnp.concatenate([toward_cot[target][column] for target in offsets], 0)
        summed.append(
            jnp.zeros((own_rows, values.shape[1]), values.dtype).at[send_index].add(values)
        )
    return tuple(summed)


def per_device(
    positions,
    tangent,
    embedding,
    counts,
    neighbours,
    send_rows,
    w_one_in,
    w_one_out,
    filter_one,
    w_left,
    w_right,
    w_two_in,
    w_two_out,
    filter_two,
    w_hidden,
    w_energy,
):
    own_rows = positions.shape[1]
    send_index = send_rows[0]
    live_rows = (jnp.arange(own_rows) < counts[0]).astype(jnp.float32)
    forward_moves = (move_bx, move_by)
    return_moves = (back_bx, back_by)
    coords_pack = jnp.concatenate([positions.T, tangent.T], 1)
    ghost_coords, ghost_embed = spread((coords_pack, embedding), send_index, forward_moves)
    phi_table = project_rows(jnp.concatenate([embedding, ghost_embed], 0), w_one_in, w_one_out)
    pos_table = jnp.concatenate([positions, ghost_coords[:, :3].T], 1)
    tan_table = jnp.concatenate([tangent, ghost_coords[:, 3:].T], 1)

    def first_section(pos_arg):
        return first_layer(pos_arg, phi_table, embedding, neighbours, filter_one, w_left, w_right)

    node_state, state_tangent = jax.jvp(first_section, (pos_table,), (tan_table,))

    def second_rows(state_arg):
        return project_rows(state_arg, w_two_in, w_two_out)

    ghost_state, ghost_state_tangent = spread(
        (node_state, state_tangent), send_index, forward_moves
    )
    state_table = jnp.concatenate([node_state, ghost_state], 0)
    state_tangents = jnp.concatenate([state_tangent, ghost_state_tangent], 0)

    def second_section(pos_arg, table_arg):
        return second_layer(
            pos_arg,
            second_rows(table_arg),
            table_arg[:own_rows],
            neighbours,
            live_rows,
            filter_two,
            w_hidden,
            w_energy,
        )

    grads_two, tangents_two = jax.jvp(
        jax.grad(second_section, argnums=(0, 1)),
        (pos_table, state_table),
        (tan_table, state_tangents),
    )
    pos_grad, pos_grad_tangent = (grads_two[0], tangents_two[0])
    ghost_pack = jnp.concatenate([pos_grad[:, own_rows:].T, pos_grad_tangent[:, own_rows:].T], 1)
    returned = gather_back(
        (grads_two[1][own_rows:], tangents_two[1][own_rows:], ghost_pack),
        send_index,
        own_rows,
        return_moves,
    )
    state_cot = grads_two[1][:own_rows] + returned[0]
    state_cot_tangent = tangents_two[1][:own_rows] + returned[1]

    def pull_first(pos_arg, cot_arg):
        pullback = jax.vjp(first_section, pos_arg)[1]
        return pullback(cot_arg)[0]

    first_grad, first_grad_tangent = jax.jvp(
        pull_first, (pos_table, state_cot), (tan_table, state_cot_tangent)
    )
    first_pack = jnp.concatenate(
        [first_grad[:, own_rows:].T, first_grad_tangent[:, own_rows:].T], 1
    )
    returned_last = gather_back((first_pack,), send_index, own_rows, return_moves)
    summed = (
        pos_grad[:, :own_rows]
        + first_grad[:, :own_rows]
        + returned[2][:, :3].T
        + returned_last[0][:, :3].T
    )
    summed_tangent = (
        pos_grad_tangent[:, :own_rows]
        + first_grad_tangent[:, :own_rows]
        + returned[2][:, 3:].T
        + returned_last[0][:, 3:].T
    )
    return (-summed, -summed_tangent)


def solution(mesh):
    placed = (
        P(None, ("bx", "by")),
        P(None, ("bx", "by")),
        P(("bx", "by"), None),
        P(("bx", "by")),
        P(None, ("bx", "by")),
        P(("bx", "by"), None),
        P(),
        P(),
        P(),
        P(),
        P(),
        P(),
        P(),
        P(),
        P(),
        P(),
    )
    return jax.shard_map(
        per_device,
        mesh=mesh,
        in_specs=placed,
        out_specs=(P(None, ("bx", "by")), P(None, ("bx", "by"))),
        check_vma=False,
    )
```

profile of v0, /device:TPU:102, one launch (start us, length us, event | category | flops | bytes accessed | tf_op | source)
XLA Modules:
  0.0 634.7 jit_solution(17414537772977224282)
XLA Ops:
  55.4 10.8 %gather_fusion.10 = f32[4096,3]{1,0:T(8,128)S(1)} fusion(f32[3,192]{0,1:T(8,128)S(1)} %copy.337, s32[4096]{0:T(1024)S(1)} %broadcast_clamp_fusion), kind=kCustom, calls=%fused_computation.1.clone | custom fusion | bytes 114688 | tf_op jit(solution)/shard_map/jvp(jvp(jit(_take)))/gather | solution.py:28
  67.6 14.2 %gather_fusion.11 = f32[4096,3]{1,0:T(8,128)} fusion(f32[3,192]{0,1:T(8,128)S(1)} %copy.367, s32[4096]{0:T(1024)S(1)} %broadcast_clamp_fusion), kind=kCustom, calls=%fused_computation.2.clone | custom fusion | bytes 114688 | tf_op jit(solution)/shard_map/jvp(jvp(jit(_take)))/gather | solution.py:28
  85.3 10.4 %fusion.186 = f32[32,128,512]{2,1,0:T(8,128)} fusion(f32[32,128]{1,0:T(8,128)S(1)} %get-tuple-element.137, f32[32,128]{1,0:T(8,128)S(1)} %get-tuple-element.110, f32[32,128]{1,0:T(8,128)S(1)} %get-tuple-element.111, f32[32,128]{1,0:T(8,128)S(1)} %get-tuple-element.138, f32[20]{0:T(128)S(1)} %copy-done.77, f32[20,512]{1,0:T(8,128)S(1)} %copy-done.33), kind=kOutput, calls=%fused_computation.265 | convolution fusion | flops 503889920 | bytes 8495184 | tf_op jit(solution)/shard_map/jvp(qkr,qc->krc)/dot_general | solution.py:41
  99.1 6.5 %fusion.188 = f32[32,128,256]{2,1,0:T(8,128)} fusion(f32[32,128]{1,0:T(8,128)S(1)} %get-tuple-element.137, f32[32,128]{1,0:T(8,128)S(1)} %get-tuple-element.110, f32[32,128]{1,0:T(8,128)S(1)} %get-tuple-element.111, f32[32,128]{1,0:T(8,128)S(1)} %get-tuple-element.138, f32[20]{0:T(128)S(1)} %copy-done.77, f32[20,256]{1,0:T(8,128)S(1)} %copy-done.52), kind=kOutput, calls=%fused_computation.266 | convolution fusion | flops 252231680 | bytes 4280400 | tf_op jit(solution)/shard_map/jvp(jvp(qkr,qc->krc))/dot_general | solution.py:41
  106.7 17.3 %collective-permute-start.7 = (f32[24,256]{1,0:T(8,128)S(1)}, f32[24,256]{1,0:T(8,128)S(1)}, u32[]{:S(2)}, u32[]{:S(2)}) collective-permute-start(f32[24,256]{1,0:T(8,128)S(1)} %pad_maximum_fusion.3), channel_id=1, source_target_pairs={{1,0},{2,1},{3,2},{4,3},{5,4},{6,5},{7,6},{8,7},{9,8},{10,9},{11,1... | collective-permute-start | bytes 73736 | tf_op jit(solution)/shard_map/ppermute | solution.py:17
  126.7 16.9 %gather_fusion.20 = f32[4096,512]{1,0:T(8,128)} fusion(f32[192,512]{1,0:T(8,128)S(1)} %fusion.176, s32[4096]{0:T(1024)S(1)} %broadcast_clamp_fusion), kind=kCustom, calls=%fused_computation.4.clone | custom fusion | bytes 16793600 | tf_op jit(solution)/shard_map/jvp(jit(_take))/gather | solution.py:48
  143.6 15.0 %add_multiply_fusion.1 = (f32[32,128,512]{2,1,0:T(8,128)S(1)}, f32[32,128,512]{2,1,0:T(8,128)S(1)}, f32[32,128,512]{2,1,0:T(8,128)}) fusion(f32[32,128,512]{2,1,0:T(8,128)} %fusion.186, f32[32,128]{1,0:T(8,128)S(1)} %get-tuple-element.109, f32[32,128]{1,0:T(8,128)S(1)} %get-tuple-element.136, pred[32,128]{1,0:T(8,128)(4,1)S(1)} %compare_and_fusion, ...), kind=kOutput, calls=%fused_computation.55 | convolution fusion | flops 518160384 | bytes 42037328 | tf_op jit(solution)/shard_map/jvp(qkr,qc->krc)/dot_general | solution.py:41
  208.6 6.0 collective-permute-start.8
  234.2 16.3 %gather_fusion.1 = f32[4096,256]{1,0:T(8,128)} fusion(f32[192,256]{1,0:T(8,128)S(1)} %fusion.163, s32[4096]{0:T(1024)S(1)} %copy-done.30), kind=kCustom, calls=%fused_computation.38 | custom fusion | bytes 8404992 | tf_op jit(solution)/shard_map/jvp(jvp(jit(_take)))/gather | solution.py:64
  250.5 16.1 %gather_fusion = f32[4096,256]{1,0:T(8,128)} fusion(f32[192,256]{1,0:T(8,128)S(1)} %fusion.174, s32[4096]{0:T(1024)S(1)} %copy-done.30), kind=kCustom, calls=%fused_computation.36 | custom fusion | bytes 8404992 | tf_op jit(solution)/shard_map/jvp(jvp(jit(_take)))/gather | solution.py:64
  266.7 11.9 %add_reduce_fusion.2 = (f32[128,256]{1,0:T(8,128)S(1)}, f32[128,256]{1,0:T(8,128)S(1)}, f32[32,128,256]{2,1,0:T(8,128)S(1)}) fusion(f32[32,128,256]{2,1,0:T(8,128)} %bitcast.231, f32[32,128,256]{2,1,0:T(8,128)} %bitcast.227, f32[32,128]{1,0:T(8,128)S(1)} %get-tuple-element.109, f32[32,128,256]{2,1,0:T(8,128)} %fusion.188, ...), kind=kOutput, calls=%fused_computation.73 | convolution fusion | flops 264339456 | bytes 17113168 | tf_op jit(solution)/shard_map/jvp(jvp(qkr,qc->krc))/dot_general | solution.py:41
  281.4 7.1 %multiply_reduce_fusion.1 = (f32[32,128]{1,0:T(8,128)}, f32[32,128]{1,0:T(8,128)}, f32[32,128,256]{2,1,0:T(8,128)}, f32[32,128,256]{2,1,0:T(8,128)}) fusion(f32[32,128,256]{2,1,0:T(8,128)S(1)} %get-tuple-element.213, f32[32,128,256]{2,1,0:T(8,128)S(1)} %bitcast.229, f32[128,256]{1,0:T(8,128)S(1)} %get-tuple-element.214, ...), kind=kLoop, calls=%fused_computation.78 | loop fusion | flops 20963328 | bytes 25497600 | tf_op jit(solution)/shard_map/jvp(transpose(jvp()))/reduce_sum | solution.py:42
  288.5 23.5 %scatter_custom_fusion.1 = f32[192,256]{1,0:T(8,128)} fusion(s32[4096]{0:T(1024)} %fusion.267, f32[4096,256]{1,0:T(8,128)} %bitcast.236, f32[]{:T(128)} %constant.59.clone.1), kind=kCustom, calls=%fused_computation.294 | custom fusion | flops 1048576 | bytes 197120 | tf_op jit(solution)/shard_map/jvp(transpose(jvp(jit(_take))))/scatter-add | solution.py:64
  315.0 23.5 %scatter_custom_fusion.6 = f32[192,256]{1,0:T(8,128)} fusion(s32[4096]{0:T(1024)} %fusion.267, f32[4096,256]{1,0:T(8,128)} %bitcast.235, f32[]{:T(128)} %constant.59.clone.1), kind=kCustom, calls=%fused_computation.292 | custom fusion | flops 1048576 | bytes 197120 | tf_op jit(solution)/shard_map/jvp(transpose(jvp(jit(_take))))/scatter-add | solution.py:64
  341.6 8.2 %fusion.7 = f32[32,128,20]{1,2,0:T(8,128)} fusion(f32[32,128,256]{2,1,0:T(8,128)} %bitcast.228, f32[32,128,256]{2,1,0:T(8,128)} %bitcast.232, f32[128,256]{1,0:T(8,128)} %copy-done.59, f32[32,128]{1,0:T(8,128)S(1)} %get-tuple-element.109, f32[128,256]{1,0:T(8,128)S(1)} %get-tuple-element.214, f32[32,128]{1,0:T(8,128)S(1)} %get-tuple-element.136, ...), kind=kOutput, calls=%fused_computation.67 | convolution fusion | flops 261095424 | bytes 9035776 | tf_op jit(solution)/shard_map/jvp(transpose(jvp(qkr,qc->krc)))/dot_general | solution.py:41
  364.9 6.0 collective-permute-start.25
  377.5 5.9 collective-permute-start.26
  388.6 8.9 %fusion.16 = f32[128,3,32]{2,1,0:T(4,128)} fusion(f32[32,128,256]{2,1,0:T(8,128)} %copy-done.8, f32[128,256,3]{1,0,2:T(8,128)S(1)} %fusion.59), kind=kOutput, calls=%fused_computation.82 | convolution fusion | flops 37748736 | bytes 4636672 | tf_op jit(solution)/shard_map/jvp(transpose(jvp(ckr,krf->crf)))/dot_general | solution.py:51
  397.5 6.8 %fusion.62 = f32[3,32,128]{1,0,2:T(4,128)} fusion(f32[32,128,256]{2,1,0:T(8,128)S(1)} %copy-done.3, f32[128,256,3]{1,0,2:T(8,128)S(1)} %fusion.59), kind=kOutput, calls=%fused_computation.121 | convolution fusion | flops 37748736 | bytes 4636672 | tf_op jit(solution)/shard_map/jvp(transpose(jvp(ckr,krf->crf)))/dot_general | solution.py:51
  420.2 6.1 fusion.68
  430.8 6.7 %fusion.6 = f32[32,128,256]{2,1,0:T(8,128)} fusion(f32[128,256,32]{1,2,0:T(8,128)S(1)} %copy-done.11, f32[128,256,32]{1,2,0:T(8,128)S(1)} %fusion.90), kind=kLoop, calls=%fused_computation.64 | loop fusion | flops 1048576 | bytes 12582912 | tf_op jit(solution)/shard_map/jvp(transpose(jvp(ckr,krf->crf)))/add_any | solution.py:51
  447.9 12.7 %fusion = f32[32,128,20]{1,2,0:T(8,128)S(1)} fusion(f32[32,128,512]{2,1,0:T(8,128)S(1)} %add_multiply_fusion.2, f32[32,128]{1,0:T(8,128)S(1)} %copy-done.38, f32[32,128]{1,0:T(8,128)S(1)} %copy-done.28, f32[32,128,256]{2,1,0:T(8,128)} %broadcast_in_dim.154, f32[32,128,256]{2,1,0:T(8,128)} %fusion.6, f32[32,128,512]{2,1,0:T(8,128)S(1)} %bitcast.226, ...), kind=kOutput, calls=%fused_computation.49 | convolution fusion | flops 515899392 | bytes 25571328 | tf_op jit(solution)/shard_map/jvp(transpose(jvp(qkr,qc->krc)))/dot_general | solution.py:41
  460.7 11.2 %fusion.97 = (f32[32,128]{1,0:T(8,128)}, f32[32,128]{1,0:T(8,128)}, f32[32,128]{1,0:T(8,128)}, f32[32,128]{1,0:T(8,128)}, f32[32,128]{1,0:T(8,128)S(1)}, /*index...) fusion(f32[32,128,20]{1,2,0:T(8,128)S(1)} %fusion, f32[32,128]{1,0:T(8,128)S(1)} %copy-done.61, ...), kind=kOutput, calls=%fused_computation.156 | convolution fusion | flops 509558784 | bytes 9642064 | tf_op jit(solution)/shard_map/jvp(transpose(jvp(qkr,qc->krc)))/dot_general | solution.py:41
  476.2 22.7 %scatter_fusion = f32[3,192]{0,1:T(8,128)S(1)} fusion(f32[3,192]{0,1:T(8,128)S(1)} %pad.30, s32[4096]{0:T(1024)S(1)} %copy-done.39, f32[4096,3]{1,0:T(8,128)} %bitcast.241), kind=kCustom, calls=%fused_computation.39 | custom fusion | flops 12288 | bytes 163840 | tf_op jit(solution)/shard_map/jvp(transpose(jvp(jit(_take))))/scatter-add | solution.py:28
  502.0 22.7 %scatter_fusion.2 = f32[3,192]{0,1:T(8,128)S(1)} fusion(f32[3,192]{0,1:T(8,128)S(1)} %pad.35, s32[4096]{0:T(1024)S(1)} %copy-done.39, f32[4096,3]{1,0:T(8,128)} %bitcast.242), kind=kCustom, calls=%fused_computation.43 | custom fusion | flops 12288 | bytes 163840 | tf_op jit(solution)/shard_map/jvp(transpose(jvp(jit(_take))))/scatter-add | solution.py:28
  528.8 6.0 collective-permute-start.21
  534.9 14.3 %multiply_reduce_fusion = (f32[32,128]{1,0:T(8,128)S(1)}, f32[32,128]{1,0:T(8,128)S(1)}) fusion(f32[32,128,512]{2,1,0:T(8,128)} %get-tuple-element.211, f32[32,128,512]{2,1,0:T(8,128)} %copy-done.5, f32[32,128,256]{2,1,0:T(8,128)} %broadcast_in_dim.154, f32[32,128,256]{2,1,0:T(8,128)} %fusion.6, f32[32,128,512]{2,1,0:T(8,128)} %bitcast.223, ...), kind=kLoop, calls=%fused_computation.58 | loop fusion | flops 18866176 | bytes 41979904 | tf_op jit(solution)/shard_map/jvp(transpose(jvp()))/reduce_sum | solution.py:42
  554.5 22.4 %scatter_fusion.1 = f32[3,192]{0,1:T(8,128)S(1)} fusion(f32[3,192]{0,1:T(8,128)S(1)} %pad.34, s32[4096]{0:T(1024)S(1)} %copy-done.39, f32[4096,3]{1,0:T(8,128)S(1)} %bitcast.238), kind=kCustom, calls=%fused_computation.42 | custom fusion | flops 12288 | bytes 163840 | tf_op jit(solution)/shard_map/jvp(transpose(jvp(jit(_take))))/scatter-add | solution.py:28
  579.0 22.4 %scatter_fusion.3 = f32[3,192]{0,1:T(8,128)S(1)} fusion(f32[3,192]{0,1:T(8,128)S(1)} %pad.39, s32[4096]{0:T(1024)S(1)} %copy-done.39, f32[4096,3]{1,0:T(8,128)S(1)} %bitcast.237), kind=kCustom, calls=%fused_computation.47 | custom fusion | flops 12288 | bytes 163840 | tf_op jit(solution)/shard_map/jvp(transpose(jvp(jit(_take))))/scatter-add | solution.py:28
  603.7 6.0 collective-permute-start.29
  610.0 6.0 collective-permute-start.22
  618.3 6.0 collective-permute-start.30
  (500 shorter events, 234.1 us)
Async XLA Ops:
  6.5 89.3 %collective-permute-start.5 = (f32[24,256]{1,0:T(8,128)S(1)}, f32[24,256]{1,0:T(8,128)}, u32[]{:S(2)}, u32[]{:S(2)}) collective-permute-start(f32[24,256]{1,0:T(8,128)S(1)} %pad_maximum_fusion.1), channel_id=1, source_target_pairs={{16,0},{32,16},{48,32},{64,48},{80,64},{96,80},{112,96},{17,1},{33... | collective-permute-start | bytes 73736 | tf_op jit(solution)/shard_map/ppermute | solution.py:17
  13.5 83.0 %collective-permute-start.4 = (f32[24,256]{1,0:T(8,128)S(1)}, f32[24,256]{1,0:T(8,128)}, u32[]{:S(2)}, u32[]{:S(2)}) collective-permute-start(f32[24,256]{1,0:T(8,128)S(1)} %pad_maximum_fusion), channel_id=1, source_target_pairs={{0,16},{16,32},{32,48},{48,64},{64,80},{80,96},{96,112},{1,17},{17... | collective-permute-start | bytes 73736 | tf_op jit(solution)/shard_map/ppermute | solution.py:17
  22.7 20.3 %collective-permute-start = (f32[24,6]{0,1:T(8,128)S(1)}, f32[24,6]{0,1:T(8,128)S(1)}, u32[]{:S(2)}, u32[]{:S(2)}) collective-permute-start(f32[24,6]{0,1:T(8,128)S(1)} %pad_maximum_fusion.21), channel_id=1, source_target_pairs={{0,16},{16,32},{32,48},{48,64},{64,80},{80,96},{96,112},{1,17},{17... | collective-permute-start | bytes 1736 | tf_op jit(solution)/shard_map/ppermute | solution.py:17
  26.3 16.9 %collective-permute-start.1 = (f32[24,6]{0,1:T(8,128)S(1)}, f32[24,6]{0,1:T(8,128)S(1)}, u32[]{:S(2)}, u32[]{:S(2)}) collective-permute-start(f32[24,6]{0,1:T(8,128)S(1)} %pad_maximum_fusion.22), channel_id=1, source_target_pairs={{16,0},{32,16},{48,32},{64,48},{80,64},{96,80},{112,96},{17,1},{33... | collective-permute-start | bytes 1736 | tf_op jit(solution)/shard_map/ppermute | solution.py:17
  43.3 5.7 collective-permute-start.3
  47.1 7.3 %collective-permute-start.2 = (f32[24,6]{0,1:T(8,128)S(1)}, f32[24,6]{0,1:T(8,128)S(1)}, u32[]{:S(2)}, u32[]{:S(2)}) collective-permute-start(f32[24,6]{0,1:T(8,128)S(1)} %pad_maximum_fusion.23), channel_id=1, source_target_pairs={{0,1},{1,2},{2,3},{3,4},{4,5},{5,6},{6,7},{7,8},{8,9},{9,10},{10,1... | collective-permute-start | bytes 1736 | tf_op jit(solution)/shard_map/ppermute | solution.py:17
  97.2 8.8 %collective-permute-start.6 = (f32[24,256]{1,0:T(8,128)S(1)}, f32[24,256]{1,0:T(8,128)S(1)}, u32[]{:S(2)}, u32[]{:S(2)}) collective-permute-start(f32[24,256]{1,0:T(8,128)S(1)} %pad_maximum_fusion.2), channel_id=1, source_target_pairs={{0,1},{1,2},{2,3},{3,4},{4,5},{5,6},{6,7},{7,8},{8,9},{9,10},{10,1... | collective-permute-start | bytes 73736 | tf_op jit(solution)/shard_map/ppermute | solution.py:17
  106.7 18.4 %collective-permute-start.7 = (f32[24,256]{1,0:T(8,128)S(1)}, f32[24,256]{1,0:T(8,128)S(1)}, u32[]{:S(2)}, u32[]{:S(2)}) collective-permute-start(f32[24,256]{1,0:T(8,128)S(1)} %pad_maximum_fusion.3), channel_id=1, source_target_pairs={{1,0},{2,1},{3,2},{4,3},{5,4},{6,5},{7,6},{8,7},{9,8},{10,9},{11,1... | collective-permute-start | bytes 73736 | tf_op jit(solution)/shard_map/ppermute | solution.py:17
  196.5 19.6 %collective-permute-start.17 = (f32[24,256]{1,0:T(8,128)S(1)}, f32[24,256]{1,0:T(8,128)S(1)}, u32[]{:S(2)}, u32[]{:S(2)}) collective-permute-start(f32[24,256]{1,0:T(8,128)S(1)} %pad_maximum_fusion.13), channel_id=1, source_target_pairs={{16,0},{32,16},{48,32},{64,48},{80,64},{96,80},{112,96},{17,1},{33... | collective-permute-start | bytes 73736 | tf_op jit(solution)/shard_map/ppermute | solution.py:17
  200.9 15.2 %collective-permute-start.16 = (f32[24,256]{1,0:T(8,128)S(1)}, f32[24,256]{1,0:T(8,128)S(1)}, u32[]{:S(2)}, u32[]{:S(2)}) collective-permute-start(f32[24,256]{1,0:T(8,128)S(1)} %pad_maximum_fusion.12), channel_id=1, source_target_pairs={{0,16},{16,32},{32,48},{48,64},{64,80},{80,96},{96,112},{1,17},{17... | collective-permute-start | bytes 73736 | tf_op jit(solution)/shard_map/ppermute | solution.py:17
  206.6 11.4 %collective-permute-start.9 = (f32[24,256]{1,0:T(8,128)S(1)}, f32[24,256]{1,0:T(8,128)S(1)}, u32[]{:S(2)}, u32[]{:S(2)}) collective-permute-start(f32[24,256]{1,0:T(8,128)S(1)} %pad_maximum_fusion.5), channel_id=1, source_target_pairs={{16,0},{32,16},{48,32},{64,48},{80,64},{96,80},{112,96},{17,1},{33... | collective-permute-start | bytes 73736 | tf_op jit(solution)/shard_map/ppermute | solution.py:17
  208.6 9.5 %collective-permute-start.8 = (f32[24,256]{1,0:T(8,128)S(1)}, f32[24,256]{1,0:T(8,128)S(1)}, u32[]{:S(2)}, u32[]{:S(2)}) collective-permute-start(f32[24,256]{1,0:T(8,128)S(1)} %pad_maximum_fusion.4), channel_id=1, source_target_pairs={{0,16},{16,32},{32,48},{48,64},{64,80},{80,96},{96,112},{1,17},{17... | collective-permute-start | bytes 73736 | tf_op jit(solution)/shard_map/ppermute | solution.py:17
  216.1 7.5 %collective-permute-start.18 = (f32[24,256]{1,0:T(8,128)S(1)}, f32[24,256]{1,0:T(8,128)S(1)}, u32[]{:S(2)}, u32[]{:S(2)}) collective-permute-start(f32[24,256]{1,0:T(8,128)S(1)} %pad_maximum_fusion.14), channel_id=1, source_target_pairs={{0,1},{1,2},{2,3},{3,4},{4,5},{5,6},{6,7},{7,8},{8,9},{9,10},{10,1... | collective-permute-start | bytes 73736 | tf_op jit(solution)/shard_map/ppermute | solution.py:17
  218.1 8.0 %collective-permute-start.10 = (f32[24,256]{1,0:T(8,128)S(1)}, f32[24,256]{1,0:T(8,128)S(1)}, u32[]{:S(2)}, u32[]{:S(2)}) collective-permute-start(f32[24,256]{1,0:T(8,128)S(1)} %pad_maximum_fusion.6), channel_id=1, source_target_pairs={{0,1},{1,2},{2,3},{3,4},{4,5},{5,6},{6,7},{7,8},{8,9},{9,10},{10,1... | collective-permute-start | bytes 73736 | tf_op jit(solution)/shard_map/ppermute | solution.py:17
  223.7 4.9 collective-permute-start.19
  226.2 3.9 collective-permute-start.11
  354.9 16.0 %collective-permute-start.12 = (f32[24,256]{1,0:T(8,128)S(1)}, f32[24,256]{1,0:T(8,128)S(1)}, u32[]{:S(2)}, u32[]{:S(2)}) collective-permute-start(f32[24,256]{1,0:T(8,128)S(1)} %pad_maximum_fusion.8), channel_id=1, source_target_pairs={{0,1},{1,2},{2,3},{3,4},{4,5},{5,6},{6,7},{7,8},{8,9},{9,10},{10,1... | collective-permute-start | bytes 73736 | tf_op jit(solution)/shard_map/ppermute | solution.py:17
  359.6 11.4 %collective-permute-start.13 = (f32[24,256]{1,0:T(8,128)S(1)}, f32[24,256]{1,0:T(8,128)S(1)}, u32[]{:S(2)}, u32[]{:S(2)}) collective-permute-start(f32[24,256]{1,0:T(8,128)S(1)} %pad_maximum_fusion.9), channel_id=1, source_target_pairs={{1,0},{2,1},{3,2},{4,3},{5,4},{6,5},{7,6},{8,7},{9,8},{10,9},{11,1... | collective-permute-start | bytes 73736 | tf_op jit(solution)/shard_map/ppermute | solution.py:17
  362.9 13.9 %collective-permute-start.24 = (f32[24,256]{1,0:T(8,128)S(1)}, f32[24,256]{1,0:T(8,128)S(1)}, u32[]{:S(2)}, u32[]{:S(2)}) collective-permute-start(f32[24,256]{1,0:T(8,128)S(1)} %pad_maximum_fusion.16), channel_id=1, source_target_pairs={{0,1},{1,2},{2,3},{3,4},{4,5},{5,6},{6,7},{7,8},{8,9},{9,10},{10,1... | collective-permute-start | bytes 73736 | tf_op jit(solution)/shard_map/ppermute | solution.py:17
  364.9 12.0 %collective-permute-start.25 = (f32[24,256]{1,0:T(8,128)S(1)}, f32[24,256]{1,0:T(8,128)S(1)}, u32[]{:S(2)}, u32[]{:S(2)}) collective-permute-start(f32[24,256]{1,0:T(8,128)S(1)} %pad_maximum_fusion.17), channel_id=1, source_target_pairs={{1,0},{2,1},{3,2},{4,3},{5,4},{6,5},{7,6},{8,7},{9,8},{10,9},{11,1... | collective-permute-start | bytes 73736 | tf_op jit(solution)/shard_map/ppermute | solution.py:17
  371.0 15.0 %collective-permute-start.14 = (f32[24,256]{1,0:T(8,128)S(1)}, f32[24,256]{1,0:T(8,128)S(1)}, u32[]{:S(2)}, u32[]{:S(2)}) collective-permute-start(f32[24,256]{1,0:T(8,128)S(1)} %pad_maximum_fusion.10), channel_id=1, source_target_pairs={{0,16},{16,32},{32,48},{48,64},{64,80},{80,96},{96,112},{1,17},{17... | collective-permute-start | bytes 73736 | tf_op jit(solution)/shard_map/ppermute | solution.py:17
  374.8 11.2 %collective-permute-start.15 = (f32[24,256]{1,0:T(8,128)S(1)}, f32[24,256]{1,0:T(8,128)S(1)}, u32[]{:S(2)}, u32[]{:S(2)}) collective-permute-start(f32[24,256]{1,0:T(8,128)S(1)} %pad_maximum_fusion.11), channel_id=1, source_target_pairs={{16,0},{32,16},{48,32},{64,48},{80,64},{96,80},{112,96},{17,1},{33... | collective-permute-start | bytes 73736 | tf_op jit(solution)/shard_map/ppermute | solution.py:17
  377.5 31.9 %collective-permute-start.26 = (f32[24,256]{1,0:T(8,128)}, f32[24,256]{1,0:T(8,128)}, u32[]{:S(2)}, u32[]{:S(2)}) collective-permute-start(f32[24,256]{1,0:T(8,128)} %pad_maximum_fusion.18), channel_id=1, source_target_pairs={{0,16},{16,32},{32,48},{48,64},{64,80},{80,96},{96,112},{1,17},{17... | collective-permute-start | bytes 73736 | tf_op jit(solution)/shard_map/ppermute | solution.py:17
  384.1 25.3 %collective-permute-start.27 = (f32[24,256]{1,0:T(8,128)}, f32[24,256]{1,0:T(8,128)S(1)}, u32[]{:S(2)}, u32[]{:S(2)}) collective-permute-start(f32[24,256]{1,0:T(8,128)} %pad_maximum_fusion.19), channel_id=1, source_target_pairs={{16,0},{32,16},{48,32},{64,48},{80,64},{96,80},{112,96},{17,1},{33... | collective-permute-start | bytes 73736 | tf_op jit(solution)/shard_map/ppermute | solution.py:17
  526.2 83.6 %collective-permute-start.20 = (f32[24,6]{0,1:T(8,128)}, f32[24,6]{0,1:T(8,128)S(1)}, u32[]{:S(2)}, u32[]{:S(2)}) collective-permute-start(f32[24,6]{0,1:T(8,128)} %pad_maximum_fusion.28), channel_id=1, source_target_pairs={{0,1},{1,2},{2,3},{3,4},{4,5},{5,6},{6,7},{7,8},{8,9},{9,10},{10,1... | collective-permute-start | bytes 1736 | tf_op jit(solution)/shard_map/ppermute | solution.py:17
  528.8 81.1 %collective-permute-start.21 = (f32[24,6]{0,1:T(8,128)}, f32[24,6]{0,1:T(8,128)S(1)}, u32[]{:S(2)}, u32[]{:S(2)}) collective-permute-start(f32[24,6]{0,1:T(8,128)} %pad_maximum_fusion.29), channel_id=1, source_target_pairs={{1,0},{2,1},{3,2},{4,3},{5,4},{6,5},{7,6},{8,7},{9,8},{10,9},{11,1... | collective-permute-start | bytes 1736 | tf_op jit(solution)/shard_map/ppermute | solution.py:17
  601.7 16.3 %collective-permute-start.28 = (f32[24,6]{0,1:T(8,128)S(1)}, f32[24,6]{0,1:T(8,128)S(1)}, u32[]{:S(2)}, u32[]{:S(2)}) collective-permute-start(f32[24,6]{0,1:T(8,128)S(1)} %pad_maximum_fusion.34), channel_id=1, source_target_pairs={{0,1},{1,2},{2,3},{3,4},{4,5},{5,6},{6,7},{7,8},{8,9},{9,10},{10,1... | collective-permute-start | bytes 1736 | tf_op jit(solution)/shard_map/ppermute | solution.py:17
  603.7 14.4 %collective-permute-start.29 = (f32[24,6]{0,1:T(8,128)S(1)}, f32[24,6]{0,1:T(8,128)S(1)}, u32[]{:S(2)}, u32[]{:S(2)}) collective-permute-start(f32[24,6]{0,1:T(8,128)S(1)} %pad_maximum_fusion.35), channel_id=1, source_target_pairs={{1,0},{2,1},{3,2},{4,3},{5,4},{6,5},{7,6},{8,7},{9,8},{10,9},{11,1... | collective-permute-start | bytes 1736 | tf_op jit(solution)/shard_map/ppermute | solution.py:17
  610.0 16.3 %collective-permute-start.22 = (f32[24,6]{0,1:T(8,128)S(1)}, f32[24,6]{0,1:T(8,128)S(1)}, u32[]{:S(2)}, u32[]{:S(2)}) collective-permute-start(f32[24,6]{0,1:T(8,128)S(1)} %pad_maximum_fusion.30), channel_id=1, source_target_pairs={{0,16},{16,32},{32,48},{48,64},{64,80},{80,96},{96,112},{1,17},{17... | collective-permute-start | bytes 1736 | tf_op jit(solution)/shard_map/ppermute | solution.py:17
  616.1 10.2 %collective-permute-start.23 = (f32[24,6]{0,1:T(8,128)S(1)}, f32[24,6]{0,1:T(8,128)S(1)}, u32[]{:S(2)}, u32[]{:S(2)}) collective-permute-start(f32[24,6]{0,1:T(8,128)S(1)} %pad_maximum_fusion.31), channel_id=1, source_target_pairs={{16,0},{32,16},{48,32},{64,48},{80,64},{96,80},{112,96},{17,1},{33... | collective-permute-start | bytes 1736 | tf_op jit(solution)/shard_map/ppermute | solution.py:17
  618.3 9.2 %collective-permute-start.30 = (f32[24,6]{0,1:T(8,128)S(1)}, f32[24,6]{0,1:T(8,128)S(1)}, u32[]{:S(2)}, u32[]{:S(2)}) collective-permute-start(f32[24,6]{0,1:T(8,128)S(1)} %pad_maximum_fusion.36), channel_id=1, source_target_pairs={{0,16},{16,32},{32,48},{48,64},{64,80},{80,96},{96,112},{1,17},{17... | collective-permute-start | bytes 1736 | tf_op jit(solution)/shard_map/ppermute | solution.py:17
  624.4 7.6 %collective-permute-start.31 = (f32[24,6]{0,1:T(8,128)S(1)}, f32[24,6]{0,1:T(8,128)S(1)}, u32[]{:S(2)}, u32[]{:S(2)}) collective-permute-start(f32[24,6]{0,1:T(8,128)S(1)} %pad_maximum_fusion.37), channel_id=1, source_target_pairs={{16,0},{32,16},{48,32},{64,48},{80,64},{96,80},{112,96},{17,1},{33... | collective-permute-start | bytes 1736 | tf_op jit(solution)/shard_map/ppermute | solution.py:17
  (92 other events, 2349.7 us)
where the time goes:
time: 646 us; the launch traced here: 635 us
  other arithmetic  200 us (31%)
  matrix products  150 us (23%)
  local copies, waits for them, and re-layouts  143 us (22%)
  starting transfers between devices  125 us (19%)
  waiting for transfers between devices  13.7 us (2%)
    ppermute x32, starting transfers between devices, passed_along(): return lax.ppermute(block, axis, route)  125 us
    scatter-add x4, other arithmetic, geometry(): others = jnp.take(pos_table, own_lists, axis=1)  90.3 us
    dot_general x8, matrix products, edge_weights(): mixed = jnp.einsum('qkr,qc->krc', radial, filter_table, precision=highest)  80.9 us
    dot_general x9, matrix products, first_layer(): jnp.einsum('ckr,krf->crf', direction, message[:, :, channels:], precision...  48.7 us
    scatter-add x2, other arithmetic, second_layer(): jnp.take(phi_table, own_lists, axis=0)  47 us
    gather x2, local copies, waits for them, and re-layouts, second_layer(): jnp.take(phi_table, own_lists, axis=0)  32.5 us
    gather x32, local copies, waits for them, and re-layouts, toward(): return tuple((jnp.take(member, chosen, axis=0) for member in payload))  31 us
    gather x4, local copies, waits for them, and re-layouts, geometry(): others = jnp.take(pos_table, own_lists, axis=1)  28.9 us
  transfers between devices with their start and end apart: 32, of which 4 were waited for; matrix products, arithmetic and copies ran while one was open for 27% of the time, Pallas kernels for 0%

commit v1 on v0

v1 whole, which is shorter than its diff:
```python
import functools
import math

import jax
import jax.numpy as jnp
from jax import lax
from jax.experimental import pallas as pl
from jax.experimental.pallas import tpu as pltpu
from jax.sharding import PartitionSpec as P

MESH = pl.DeviceIdType.MESH
f32 = jnp.float32
bf16 = jnp.bfloat16
offsets = ((-1, -1), (-1, 0), (-1, 1), (0, -1), (0, 1), (1, -1), (1, 0), (1, 1))
NN = (((1,), (0,)), ((), ()))
NT = (((1,), (1,)), ((), ()))
KAPPA = math.pi / 3.0
SOFT = 0.01
ROWS = 128
GHOSTS = 64
TABLE = ROWS + GHOSTS
F = 256
NR = 20
PAIRS = NR // 2
SPAN = 3 * ROWS
WIDE = PAIRS * SPAN
STEP = 768
STEPS = WIDE // STEP


def split(x):
    hi = x.astype(bf16)
    return hi, (x - hi.astype(f32)).astype(bf16)


def split3(x):
    hi = x.astype(bf16)
    rest = x - hi.astype(f32)
    mid = rest.astype(bf16)
    return hi, mid, (rest - mid.astype(f32)).astype(bf16)


def mm(a, b, dims=NN):
    return lax.dot_general(a, b, dims, preferred_element_type=f32)


def mm3(a, b, dims=NN):
    return mm(a[0], b[0], dims) + (mm(a[1], b[0], dims) + mm(a[0], b[1], dims))


def pick(refs, *index):
    return refs[0][index], refs[1][index]


def put(refs, value, *index):
    hi, lo = split(value)
    refs[0][index] = hi
    refs[1][index] = lo


def sin_cos(angle):
    turns = jnp.floor(angle * (0.5 / math.pi) + 0.5)
    half = 0.5 * ((angle - turns * 6.28125) - turns * (2.0 * math.pi - 6.28125))
    sq = half * half
    odd = 1.0 / 39916800.0
    for c in (1.0 / 362880.0, 1.0 / 5040.0, 1.0 / 120.0, 1.0 / 6.0, 1.0):
        odd = c - sq * odd
    sh = half * odd
    even = 1.0 / 479001600.0
    for c in (1.0 / 3628800.0, 1.0 / 40320.0, 1.0 / 720.0, 1.0 / 24.0, 0.5, 1.0):
        even = c - sq * even
    return 2.0 * sh * even, 1.0 - 2.0 * sh * sh


def sigmoid(v):
    return 1.0 / (1.0 + jnp.exp(-v))


def own_waves(s1, c1):
    twice = 2.0 * c1
    before_s, before_c = jnp.zeros_like(s1), jnp.ones_like(c1)
    s, c = s1, c1
    for q in range(NR):
        yield (q // 2) * SPAN + (q % 2) * ROWS, (q + 1) * KAPPA, s, c
        if q < NR - 1:
            s, before_s = twice * s - before_s, s
            c, before_c = twice * c - before_c, c


def ghost_waves(s1, c1):
    upper = lax.broadcasted_iota(jnp.int32, s1.shape, 1) >= GHOSTS
    s2, c2 = 2.0 * s1 * c1, 1.0 - 2.0 * s1 * s1
    twice = 2.0 * c2
    s, before_s = jnp.where(upper, s2, s1), jnp.where(upper, 0.0, -s1)
    c, before_c = jnp.where(upper, c2, c1), jnp.where(upper, 1.0, c1)
    shift = jnp.where(upper, 2.0 * KAPPA, KAPPA)
    for p in range(PAIRS):
        yield p * SPAN + 2 * ROWS, shift + 2.0 * p * KAPPA, s, c
        if p < PAIRS - 1:
            s, before_s = twice * s - before_s, s
            c, before_c = twice * c - before_c, c


E0, E1, E2, DD, IV, S1, C1, U0, W0 = 0, 1, 2, 3, 4, 5, 6, 7, 10
WAVES = (own_waves, ghost_waves)


def kernel(
    nx,
    ny,
    pos,
    tan,
    emb,
    cnt,
    nbr,
    snd,
    w1i,
    w1o,
    f1,
    wl,
    wr,
    w2i,
    w2o,
    f2,
    wh,
    we,
    force,
    hess,
    w1i_s,
    w1o_s,
    wlr_s,
    w2i_s,
    w2o_s,
    wh_s,
    sndpad,
    c8,
    csel,
    crecv,
    sel1,
    gemb,
    sel2,
    gnode,
    src3,
    rnode,
    gpos,
    rpos,
    onehot,
    mask,
    colb,
    geo,
    lbh,
    lbl,
    lvh,
    lvl,
    lth,
    ltl,
    pfs_s,
    pfv_s,
    p2_s,
    p2d_s,
    phi,
    acc,
    lr,
    node,
    pre2,
    phi2,
    mu,
    bar,
    out,
    pg,
    send1,
    recv1,
    sendc,
    recvc,
    send2,
    recv2,
    send3,
    recv3,
    send4,
    recv4,
    loads,
):
    lb, lv, lt = (lbh, lbl), (lvh, lvl), (lth, ltl)
    ix, iy = lax.axis_index("bx"), lax.axis_index("by")

    def device(g, sign):
        dx, dy = offsets[g]
        return (lax.rem(ix + sign * dx + nx, nx), lax.rem(iy + sign * dy + ny, ny))

    barrier = pltpu.get_barrier_semaphore()
    for g in range(8):
        pl.semaphore_signal(barrier, inc=1, device_id=device(g, 1), device_id_type=MESH)

    def block(ref, g):
        return ref.at[pl.ds(g * 8, 8), :]

    def copies(source, target, sends, recvs, sign, whole):
        return [
            pltpu.make_async_remote_copy(
                src_ref=source if whole else block(source, g),
                dst_ref=target.at[g] if whole else block(target, g),
                send_sem=sends.at[g],
                recv_sem=recvs.at[g],
                device_id=device(g, sign),
                device_id_type=MESH,
            )
            for g in range(8)
        ]

    def select(x):
        hi, lo = split(x)
        rows = onehot[1, 0:GHOSTS, :].astype(bf16)
        return mm(rows, hi) + mm(rows, lo)

    lane = lax.broadcasted_iota(jnp.int32, (8, ROWS), 1)
    group = lax.div(lane, 8)

    def merged(ref):
        total = jnp.where(group == 0, ref[0], 0.0)
        for g in range(1, 8):
            total = total + jnp.where(group == g, ref[g], 0.0)
        return total

    weights, at = [], 0
    for number, w in enumerate((w1i, w1o, wl, wr, w2i, w2o, wh)):
        place = out.at[0:F, at : at + w.shape[1]]
        weights.append((pltpu.make_async_copy(w, place, loads.at[number]), place))
        at += w.shape[1]
    for copy, _ in weights:
        copy.start()

    sndpad[...] = jnp.full((8, ROWS), -1, jnp.int32)
    sndpad[0:1, 0:GHOSTS] = snd[...]
    hot = jnp.where(
        lax.broadcasted_iota(jnp.int32, (ROWS, ROWS), 0) == sndpad[0:1, :], 1.0, 0.0
    )
    onehot[0] = hot
    onehot[1] = hot.T
    c8[...] = jnp.zeros((8, ROWS), f32)
    c8[0:3, :] = pos[...]
    c8[3:6, :] = tan[...]
    hi, mid, lo = split3(c8[...])
    hot16 = hot.astype(bf16)
    csel[...] = mm(hi, hot16) + (mm(mid, hot16) + mm(lo, hot16))
    sel1[...] = select(emb[...])
    pl.semaphore_wait(barrier, 8)
    coords = copies(csel, crecv, sendc, recvc, 1, True)
    first = copies(sel1, gemb, send1, recv1, 1, False)
    for copy in coords + first:
        copy.start()

    stores = ((w1i_s, 0), (w1o_s, 0), (wlr_s, 0), (wlr_s, F), (w2i_s, 0), (w2o_s, 0), (wh_s, 0))
    for (refs, at), (copy, place) in zip(stores, weights):
        copy.wait()
        hi, lo = split(place[...])
        refs[0, :, at : at + hi.shape[1]] = hi
        refs[1, :, at : at + hi.shape[1]] = lo

    row = lax.broadcasted_iota(jnp.int32, (ROWS, ROWS), 0)
    ghost = lax.rem(row, GHOSTS)
    for side, slots in ((0, row), (1, ROWS + (7 - lax.div(ghost, 8)) * 8 + lax.rem(ghost, 8))):

        def mark(k, total, slots=slots):
            return jnp.where(slots == nbr[pl.ds(k, 1), :], 1.0, total)

        listed = lax.fori_loop(0, nbr.shape[0], mark, jnp.zeros((ROWS, ROWS), f32))
        mask[side] = listed.T

    def project(rows, first_w, second_w):
        v = mm3(split(rows), first_w)
        return mm3(split(v * sigmoid(v)), second_w)

    w1 = (w1i_s[0], w1i_s[1]), (w1o_s[0], w1o_s[1])
    phi[0:ROWS, :] = project(emb[...], *w1)
    for j in range(6):
        colb[j] = jnp.broadcast_to(c8[j : j + 1, :], (ROWS, ROWS)).T

    for copy in coords + first:
        copy.wait()
    phi[ROWS:TABLE, :] = project(gemb[...], *w1)
    found = merged(crecv)
    twofold = found + pltpu.roll(found, GHOSTS, 1)
    csel2 = (c8[...], twofold)

    scale = 1.0 / math.sqrt(nbr.shape[0])

    def geometry(i, carry):
        rows = pl.ds(pl.multiple_of(i * 8, 8), 8)
        centre = [colb[j, rows, :] for j in range(6)]
        for side in range(2):
            table = csel2[side]
            off = [table[j : j + 1, :] - centre[j] for j in range(3)]
            vel = [table[j : j + 1, :] - centre[j] for j in range(3, 6)]
            listed = mask[side, rows, :]
            sq = off[0] * off[0] + off[1] * off[1] + off[2] * off[2]
            sq = jnp.where(listed > 0.0, sq, 1.0) + SOFT
            inv = lax.rsqrt(sq)
            inv = inv * (1.5 - 0.5 * sq * inv * inv)
            dist = sq * inv
            unit = [x * inv for x in off]
            rate = unit[0] * vel[0] + unit[1] * vel[1] + unit[2] * vel[2]
            s1, c1 = sin_cos(KAPPA * dist)
            weight = scale * listed
            env = 0.5 * (c1 + 1.0)
            env1 = (-0.5 * KAPPA) * s1
            env2 = (-0.5 * KAPPA * KAPPA) * c1
            e0 = weight * env * inv
            slope = env1 - env * inv
            e1 = weight * inv * slope
            e2 = weight * inv * (env2 - 2.0 * inv * slope)
            planes = [e0, e1, e2, rate, inv, s1, c1] + unit
            planes += [(vel[j] - unit[j] * rate) * inv for j in range(3)]
            for number, value in enumerate(planes):
                geo[side, number, rows, :] = value
        return carry

    lax.fori_loop(0, ROWS // 8, geometry, 0)

    def spread_table(refs, table, filters, at):
        def body(p, carry):
            for half in range(2):
                weights = filters[pl.ds(2 * p + half, 1), at : at + F]
                start = pl.multiple_of(p * SPAN + half * ROWS, ROWS)
                hi, lo = split(table(0, ROWS) * weights)
                refs[0, pl.ds(start, ROWS), :] = hi
                refs[1, pl.ds(start, ROWS), :] = lo
                start = pl.multiple_of(p * SPAN + 2 * ROWS + half * GHOSTS, GHOSTS)
                hi, lo = split(table(ROWS, GHOSTS) * weights)
                refs[0, pl.ds(start, GHOSTS), :] = hi
                refs[1, pl.ds(start, GHOSTS), :] = lo
            return carry

        lax.fori_loop(0, PAIRS, body, 0)

    spread_table(pfs_s, lambda at, n: phi[at : at + n, 0:F], f1, 0)
    spread_table(pfv_s, lambda at, n: phi[at : at + n, F : 2 * F], f1, F)

    def pair_rows(i, carry):
        start = pl.multiple_of(i * 16, 16)
        rows = pl.ds(start, 16)
        for side in range(2):
            g = [geo[side, number, rows, :] for number in range(13)]
            e1d, e0d = g[E1] * g[DD], g[E0] * g[DD]
            for at, a, s, c in WAVES[side](g[S1], g[C1]):
                cols = slice(at, at + ROWS)
                b = g[E0] * s
                bd = e1d * s + e0d * (a * c)
                put(lb, b, rows, cols)
                put(lb, bd, pl.ds(start + ROWS, 16), cols)
                for j in range(3):
                    put(lv, b * g[U0 + j], pl.ds(start + j * ROWS, 16), cols)
                    put(
                        lv,
                        bd * g[U0 + j] + b * g[W0 + j],
                        pl.ds(start + (3 + j) * ROWS, 16),
                        cols,
                    )
        return carry

    lax.fori_loop(0, ROWS // 16, pair_rows, 0)

    def gather_messages(target, left, rows, right):
        def body(i, carry):
            cols = pl.ds(pl.multiple_of(i * STEP, STEP), STEP)
            b = right[0, cols, :], right[1, cols, :]
            target[0:rows, :] += mm3((left[0][0:rows, cols], left[1][0:rows, cols]), b)
            return carry

        target[0:rows, :] = jnp.zeros((rows, F), f32)
        lax.fori_loop(0, STEPS, body, 0)

    gather_messages(acc, lv, 6 * ROWS, pfv_s)
    lr[...] = mm3(split(acc[...]), (wlr_s[0], wlr_s[1]))
    gather_messages(acc, lb, 2 * ROWS, pfs_s)

    def part(j, side):
        return lr[j * ROWS : (j + 1) * ROWS, side * F : (side + 1) * F]

    state = emb[...] + acc[0:ROWS, :]
    moved = acc[ROWS : 2 * ROWS, :]
    for j in range(3):
        state = state + part(j, 0) * part(j, 1)
        moved = moved + (part(3 + j, 0) * part(j, 1) + part(j, 0) * part(3 + j, 1))
    node[:, 0:F] = state
    node[:, F : 2 * F] = moved
    sel2[...] = select(node[...])
    second = copies(sel2, gnode, send2, recv2, 1, False)
    for copy in second:
        copy.start()

    w2 = (w2i_s[0], w2i_s[1]), (w2o_s[0], w2o_s[1])

    def table_two(values, moves, at, n):
        v = mm3(split(values), w2[0])
        vd = mm3(split(moves), w2[0])
        sig = sigmoid(v)
        pre2[0, at : at + n, :] = v
        pre2[1, at : at + n, :] = vd
        slope = sig * (1.0 + v * (1.0 - sig))
        phi2[0, at : at + n, :] = mm3(split(v * sig), w2[1])
        phi2[1, at : at + n, :] = mm3(split(slope * vd), w2[1])

    table_two(node[:, 0:F], node[:, F : 2 * F], 0, ROWS)

    for side in range(2):
        rows = ROWS if side == 0 else GHOSTS
        e0, e1, rate = (geo[side, number] for number in (E0, E1, DD))
        pg[side, 0] = e0.T
        pg[side, 1] = (e1 * rate).T
        pg[side, 2] = (e0 * rate).T
        pg[side, 3] = geo[side, S1].T
        pg[side, 4] = geo[side, C1].T

    def turned(side, count):
        def body(i, carry):
            start = pl.multiple_of(i * 16, 16)
            g = [pg[side, number, pl.ds(start, 16), :] for number in range(5)]
            for q, (at, a, s, c) in enumerate(own_waves(g[3], g[4])):
                cols = slice(q * ROWS, (q + 1) * ROWS)
                put(lt, g[0] * s, pl.ds(start + side * ROWS, 16), cols)
                put(
                    lt,
                    g[1] * s + g[2] * (a * c),
                    pl.ds(start + side * ROWS + TABLE, 16),
                    cols,
                )
            return carry

        lax.fori_loop(0, count // 16, body, 0)

    turned(0, ROWS)
    turned(1, GHOSTS)

    for copy in second:
        copy.wait()
    table_two(gnode[:, 0:F], gnode[:, F : 2 * F], ROWS, GHOSTS)
    spread_table(p2_s, lambda at, n: phi2[0, at : at + n, :], f2, 0)
    spread_table(p2d_s, lambda at, n: phi2[1, at : at + n, :], f2, 0)
    gather_messages(acc, lb, 2 * ROWS, p2_s)
    st = node[:, 0:F] + acc[0:ROWS, :]
    std = node[:, F : 2 * F] + acc[ROWS : 2 * ROWS, :]
    gather_messages(acc, lb, ROWS, p2d_s)
    std = std + acc[0:ROWS, :]

    whs = wh_s[0], wh_s[1]
    v = mm3(split(st), whs)
    vd = mm3(split(std), whs)
    sig = sigmoid(v)
    live = lax.broadcasted_iota(jnp.int32, (ROWS, F), 0) < cnt[0]
    top = jnp.where(live, jnp.broadcast_to(we[...], (ROWS, F)), 0.0)
    mu[0] = mm3(split(top * (sig * (1.0 + v * (1.0 - sig)))), whs, NT)
    mu[1] = mm3(
        split(top * (sig * (1.0 - sig) * (2.0 + v * (1.0 - 2.0 * sig))) * vd), whs, NT
    )

    for q in range(NR):
        weights = f2[q : q + 1, :]
        rows = slice(q % 4 * ROWS, (q % 4 + 1) * ROWS)
        for number in range(2):
            at = (number * NR // 4 + q // 4) * F
            put(lv, mu[number] * weights, rows, slice(at, at + F))
    bar[...] = jnp.zeros((2 * TABLE, F), f32)

    def turned_messages(i, carry):
        cols = pl.ds(pl.multiple_of(i * 512, 512), 512)
        place = pl.ds(pl.multiple_of(i * F, F), F)
        b = lvh[0 : 4 * ROWS, place], lvl[0 : 4 * ROWS, place]
        bar[...] += mm3((lth[:, cols], ltl[:, cols]), b)
        place = pl.ds(pl.multiple_of((NR // 4 + i) * F, F), F)
        b = lvh[0 : 4 * ROWS, place], lvl[0 : 4 * ROWS, place]
        bar[TABLE : 2 * TABLE, :] += mm3((lth[0:TABLE, cols], ltl[0:TABLE, cols]), b)
        return carry

    lax.fori_loop(0, NR * ROWS // 512, turned_messages, 0)
    back = mm3(split(bar[...]), w2[1], NT)
    v, vd = pre2[0], pre2[1]
    sig = sigmoid(v)
    slope = sig * (1.0 + v * (1.0 - sig))
    curve = sig * (1.0 - sig) * (2.0 + v * (1.0 - 2.0 * sig))
    bar[0:TABLE, :] = back[0:TABLE] * slope
    bar[TABLE : 2 * TABLE, :] = back[TABLE : 2 * TABLE] * slope + back[0:TABLE] * curve * vd
    bar[...] = mm3(split(bar[...]), w2[0], NT)
    src3[:, 0:F] = bar[ROWS:TABLE, :]
    src3[:, F : 2 * F] = bar[TABLE + ROWS : 2 * TABLE, :]
    third = copies(src3, rnode, send3, recv3, -1, False)
    for copy in third:
        copy.start()

    m = split(mu[0])
    md = split(mu[1])

    def pairs_two(i, carry):
        cols = pl.ds(pl.multiple_of(i * STEP, STEP), STEP)
        b = p2_s[0, cols, :], p2_s[1, cols, :]
        bd = p2d_s[0, cols, :], p2d_s[1, cols, :]
        out[0:ROWS, cols] = mm3(m, b, NT)
        out[ROWS : 2 * ROWS, cols] = mm3(md, b, NT) + mm3(m, bd, NT)
        return carry

    lax.fori_loop(0, STEPS, pairs_two, 0)

    for copy in third:
        copy.wait()
    rows_back = onehot[0, :, 0:GHOSTS].astype(bf16)
    hi, lo = split(rnode[...])
    returned = mm(rows_back, hi) + mm(rows_back, lo)
    nu = mu[0] + bar[0:ROWS, :] + returned[:, 0:F]
    nud = mu[1] + bar[TABLE : TABLE + ROWS, :] + returned[:, F : 2 * F]
    mu[0] = nu
    mu[1] = nud

    wlr = wlr_s[0], wlr_s[1]
    for j in range(3):
        nu, nud = mu[0], mu[1]
        l, r, ld, rd = part(j, 0), part(j, 1), part(3 + j, 0), part(3 + j, 1)
        lr[j * ROWS : (j + 1) * ROWS, 0:F] = nu * r
        lr[j * ROWS : (j + 1) * ROWS, F : 2 * F] = nu * l
        lr[(3 + j) * ROWS : (4 + j) * ROWS, 0:F] = nud * r + nu * rd
        lr[(3 + j) * ROWS : (4 + j) * ROWS, F : 2 * F] = nud * l + nu * ld
    acc[...] = mm3(split(lr[...]), wlr, NT)
    n = split(jnp.concatenate([mu[0], mu[1]], 0))
    vb = split(acc[...])
    lvb = lv[0].at[:, 0:F], lv[1].at[:, 0:F]
    lvb[0][...] = vb[0]
    lvb[1][...] = vb[1]

    def pairs_one(i, carry):
        cols = pl.ds(pl.multiple_of(i * STEP, STEP), STEP)
        out[0 : 2 * ROWS, cols] += mm3(n, (pfs_s[0, cols, :], pfs_s[1, cols, :]), NT)
        out[2 * ROWS :, cols] = mm3(
            (lvb[0][...], lvb[1][...]), (pfv_s[0, cols, :], pfv_s[1, cols, :]), NT
        )
        return carry

    lax.fori_loop(0, STEPS, pairs_one, 0)

    def offsets_back(i, carry):
        start = pl.multiple_of(i * 8, 8)
        rows = pl.ds(start, 8)
        for side in range(2):
            zero = jnp.zeros((8, ROWS), f32)
            z = [[zero] * 4 for _ in range(3)]
            zd = [[zero] * 4 for _ in range(2)]
            for at, a, s, c in WAVES[side](geo[side, S1, rows, :], geo[side, C1, rows, :]):
                cols = slice(at, at + ROWS)
                ac = a * c
                aas = a * (a * s)
                for k in range(4):
                    y = out[pl.ds(start + (0 if k == 3 else 2 + k) * ROWS, 8), cols]
                    yd = out[pl.ds(start + (1 if k == 3 else 5 + k) * ROWS, 8), cols]
                    z[0][k] = z[0][k] + s * y
                    z[1][k] = z[1][k] + ac * y
                    z[2][k] = z[2][k] + aas * y
                    zd[0][k] = zd[0][k] + s * yd
                    zd[1][k] = zd[1][k] + ac * yd
            e0, e1, e2, rate, inv = (geo[side, number, rows, :] for number in range(5))
            unit = [geo[side, U0 + j, rows, :] for j in range(3)]
            turn = [geo[side, W0 + j, rows, :] for j in range(3)]
            a_, ad, ub, ubd = [], [], [], []
            for k in range(4):
                first_d = e1 * z[0][k] + e0 * z[1][k]
                second_d = e2 * z[0][k] + 2.0 * e1 * z[1][k] - e0 * z[2][k]
                a_.append(first_d)
                ad.append(rate * second_d + e1 * zd[0][k] + e0 * zd[1][k])
                if k < 3:
                    ub.append(e0 * z[0][k])
                    ubd.append(rate * first_d + e0 * zd[0][k])
            db, dbd, w, wd = a_[3], ad[3], zero, zero
            for j in range(3):
                db = db + unit[j] * a_[j]
                dbd = dbd + turn[j] * a_[j] + unit[j] * ad[j]
                w = w + unit[j] * ub[j]
                wd = wd + turn[j] * ub[j] + unit[j] * ubd[j]
            for j in range(3):
                t = (ub[j] - unit[j] * w) * inv
                pg[side, j, rows, :] = db * unit[j] + t
                pg[side, 3 + j, rows, :] = (
                    dbd * unit[j]
                    + db * turn[j]
                    + (ubd[j] - turn[j] * w - unit[j] * wd - t * rate) * inv
                )
        return carry

    lax.fori_loop(0, ROWS // 8, offsets_back, 0)

    gpos[...] = jnp.zeros((8, ROWS), f32)
    c8[...] = jnp.zeros((8, ROWS), f32)
    for j in range(6):
        ghosts = pg[1, j]
        own = pg[0, j]
        halves = jnp.sum(ghosts, axis=0, keepdims=True)
        gpos[j : j + 1, :] = halves
        c8[j : j + 1, :] = jnp.sum(own - own.T - ghosts.T, axis=0, keepdims=True)
    both = gpos[...]
    gpos[...] = both + pltpu.roll(both, GHOSTS, 1)
    last = copies(gpos, rpos, send4, recv4, -1, True)
    for copy in last:
        copy.start()
    for copy in last:
        copy.wait()
    hi, mid, lo = split3(merged(rpos))
    slots = onehot[1].astype(bf16)
    total = c8[...] + (mm(hi, slots) + (mm(mid, slots) + mm(lo, slots)))
    force[...] = -total[0:3, :]
    hess[...] = -total[3:6, :]


def per_device(nx, ny, *arrays):
    arrays = list(arrays)
    arrays[15] = arrays[15].reshape(1, F)
    vmem = pl.BlockSpec(memory_space=pltpu.VMEM)
    in_specs = [vmem] * 16
    in_specs[3] = pl.BlockSpec(memory_space=pltpu.SMEM)
    for number in (6, 7, 9, 10, 11, 12, 14):
        in_specs[number] = pl.BlockSpec(memory_space=pl.ANY)

    def v32(*shape):
        return pltpu.VMEM(shape, f32)

    def v16(*shape):
        return pltpu.VMEM(shape, bf16)

    dma = pltpu.SemaphoreType.DMA((8,))
    scratch = [
        v16(2, F, F),
        v16(2, F, 2 * F),
        v16(2, F, 2 * F),
        v16(2, F, F),
        v16(2, F, F),
        v16(2, F, F),
        pltpu.VMEM((8, ROWS), jnp.int32),
        v32(8, ROWS),
        v32(8, ROWS),
        v32(8, 8, ROWS),
        v32(GHOSTS, F),
        v32(GHOSTS, F),
        v32(GHOSTS, 2 * F),
        v32(GHOSTS, 2 * F),
        v32(GHOSTS, 2 * F),
        v32(GHOSTS, 2 * F),
        v32(8, ROWS),
        v32(8, 8, ROWS),
        v32(2, ROWS, ROWS),
        v32(2, ROWS, ROWS),
        v32(6, ROWS, ROWS),
        v32(2, 13, ROWS, ROWS),
        v16(2 * ROWS, WIDE),
        v16(2 * ROWS, WIDE),
        v16(6 * ROWS, WIDE),
        v16(6 * ROWS, WIDE),
        v16(2 * TABLE, NR * ROWS),
        v16(2 * TABLE, NR * ROWS),
        v16(2, WIDE, F),
        v16(2, WIDE, F),
        v16(2, WIDE, F),
        v16(2, WIDE, F),
        v32(TABLE, 2 * F),
        v32(6 * ROWS, F),
        v32(6 * ROWS, 2 * F),
        v32(ROWS, 2 * F),
        v32(2, TABLE, F),
        v32(2, TABLE, F),
        v32(2, ROWS, F),
        v32(2 * TABLE, F),
        v32(8 * ROWS, WIDE),
        v32(2, 6, ROWS, ROWS),
    ] + [dma] * 11
    out = jax.ShapeDtypeStruct((3, ROWS), f32)
    return pl.pallas_call(
        functools.partial(kernel, nx, ny),
        out_shape=(out, out),
        in_specs=in_specs,
        out_specs=(vmem, vmem),
        scratch_shapes=scratch,
        compiler_params=pltpu.CompilerParams(
            collective_id=0, has_side_effects=True, vmem_limit_bytes=67043328
        ),
    )(*arrays)


def solution(mesh):
    placed = (
        P(None, ("bx", "by")),
        P(None, ("bx", "by")),
        P(("bx", "by"), None),
        P(("bx", "by")),
        P(None, ("bx", "by")),
        P(("bx", "by"), None),
    ) + (P(),) * 10
    return jax.shard_map(
        functools.partial(per_device, mesh.shape["bx"], mesh.shape["by"]),
        mesh=mesh,
        in_specs=placed,
        out_specs=(P(None, ("bx", "by")), P(None, ("bx", "by"))),
        check_vma=False,
    )
```

time: 646 us -> 75.7 us (0.12)
  the two profiles are of different devices: /device:TPU:102 before, /device:TPU:0 now
where the time goes in v1:
time: 75.7 us; the launch traced here: 75.5 us
  Pallas kernels  72.3 us (96%)
  local copies, waits for them, and re-layouts  1.89 us (2%)
  between operations  1.3 us (2%)
    pallas_call x1, Pallas kernels, per_device(): pl.pallas_call(functools.partial(kernel, nx, ny), out_shape=(out, out), i...  72.3 us
    unnamed x6, local copies, waits for them, and re-layouts  1.89 us

profile of v1, /device:TPU:0, one launch (start us, length us, event | category | flops | bytes accessed | tf_op | source)
XLA Modules:
  0.0 75.5 jit_solution(12370577154751385768)
XLA Ops:
  1.3 72.3 %shard_map.167 = (f32[3,128]{1,0:T(4,128)}, f32[3,128]{1,0:T(4,128)}) custom-call(f32[3,128]{1,0:T(4,128)} %pos.1, f32[3,128]{1,0:T(4,128)} %tan.1, f32[128,256]{1,0:T(8,128)} %emb.1, s32[1]{0:T(128)S(6)} %copy.20.cnt, s32[32,128]{1,0:T(8,128)} %nbr.1, s32[1,64]{1,0:T(1,128)} %snd.1, f32[256,256]{1,0:T(8,128)} %w1i.1, f32[256,512]{1,0:T(8,128)} %w1o.1, ...), custom_call_target="tpu_custom_call" | custom-call | tf_op jit(solution)/shard_map/pallas_call | solution.py:669
  73.6 0.0 copy-start.1
  73.6 0.7 copy-done.1
  74.3 0.0 copy-start
  74.3 0.6 copy.21
  74.8 0.1 copy-done
  74.9 0.6 copy.22
Async XLA Ops:
  73.6 0.7 copy-start.1
  74.3 0.7 copy-start

commit v2 on v1

--- a/solution.py
+++ b/solution.py
@@ -22,9 +22,10 @@
 F = 256
 NR = 20
 PAIRS = NR // 2
-SPAN = 3 * ROWS
-WIDE = PAIRS * SPAN
-STEP = 768
+TILE = 256
+TILES = NR * TABLE // TILE
+WIDE = TILES * TILE
+STEP = 3 * TILE
 STEPS = WIDE // STEP
 
 
@@ -81,7 +82,7 @@
     before_s, before_c = jnp.zeros_like(s1), jnp.ones_like(c1)
     s, c = s1, c1
     for q in range(NR):
-        yield (q // 2) * SPAN + (q % 2) * ROWS, (q + 1) * KAPPA, s, c
+        yield (q + 1) * KAPPA, s, c
         if q < NR - 1:
             s, before_s = twice * s - before_s, s
             c, before_c = twice * c - before_c, c
@@ -95,7 +96,7 @@
     c, before_c = jnp.where(upper, c2, c1), jnp.where(upper, 1.0, c1)
     shift = jnp.where(upper, 2.0 * KAPPA, KAPPA)
     for p in range(PAIRS):
-        yield p * SPAN + 2 * ROWS, shift + 2.0 * p * KAPPA, s, c
+        yield shift + 2.0 * p * KAPPA, s, c
         if p < PAIRS - 1:
             s, before_s = twice * s - before_s, s
             c, before_c = twice * c - before_c, c
@@ -148,25 +149,33 @@
     mask,
     colb,
     geo,
-    lbh,
-    lbl,
-    lvh,
-    lvl,
-    lth,
-    ltl,
+    waves,
+    lb,
+    lv0,
+    lv1,
+    lt,
     pfs_s,
     pfv_s,
     p2_s,
     p2d_s,
+    muf0,
+    muf1,
     phi,
     acc,
+    accv,
     lr,
     node,
     pre2,
     phi2,
     mu,
     bar,
-    out,
+    out0,
+    out1,
+    landing,
+    two,
+    sums,
+    vbar,
+    nus,
     pg,
     send1,
     recv1,
@@ -180,7 +189,6 @@
     recv4,
     loads,
 ):
-    lb, lv, lt = (lbh, lbl), (lvh, lvl), (lth, ltl)
     ix, iy = lax.axis_index("bx"), lax.axis_index("by")
 
     def device(g, sign):
@@ -221,11 +229,11 @@
             total = total + jnp.where(group == g, ref[g], 0.0)
         return total
 
-    weights, at = [], 0
-    for number, w in enumerate((w1i, w1o, wl, wr, w2i, w2o, wh)):
-        place = out.at[0:F, at : at + w.shape[1]]
+    weights = []
+    spots = ((0, 0), (0, F), (1, 0), (1, F), (1, 2 * F), (2, 0), (2, F))
+    for number, (w, (down, at)) in enumerate(zip((w1i, w1o, wl, wr, w2i, w2o, wh), spots)):
+        place = landing.at[down * F : (down + 1) * F, at : at + w.shape[1]]
         weights.append((pltpu.make_async_copy(w, place, loads.at[number]), place))
-        at += w.shape[1]
     for copy, _ in weights:
         copy.start()
 
@@ -275,12 +283,44 @@
     for j in range(6):
         colb[j] = jnp.broadcast_to(c8[j : j + 1, :], (ROWS, ROWS)).T
 
+    def put2(refs, value, start):
+        hi, lo = split(value)
+        refs[0, pl.ds(start, value.shape[0]), :] = hi
+        refs[1, pl.ds(start, value.shape[0]), :] = lo
+
+    def spread_own(refs, table, filters, at):
+        def body(q, carry):
+            weights = filters[pl.ds(q, 1), at : at + F]
+            put2(refs, table() * weights, pl.multiple_of(q * ROWS, ROWS))
+            return carry
+
+        lax.fori_loop(0, NR, body, 0)
+
+    def spread_ghosts(refs, table, filters, at):
+        def body(q, carry):
+            weights = filters[pl.ds(q, 1), at : at + F]
+            put2(refs, table() * weights, pl.multiple_of(NR * ROWS + q * GHOSTS, GHOSTS))
+            return carry
+
+        lax.fori_loop(0, NR, body, 0)
+
+    def put_rows(ref, value, first, second, cols):
+        hi, lo = split(value)
+        ref[first : first + 16, cols] = hi
+        ref[second : second + 16, cols] = lo
+
+    spread_own(pfs_s, lambda: phi[0:ROWS, 0:F], f1, 0)
+    spread_own(pfv_s, lambda: phi[0:ROWS, F : 2 * F], f1, F)
+
     for copy in coords + first:
         copy.wait()
     phi[ROWS:TABLE, :] = project(gemb[...], *w1)
     found = merged(crecv)
     twofold = found + pltpu.roll(found, GHOSTS, 1)
     csel2 = (c8[...], twofold)
+
+    spread_ghosts(pfs_s, lambda: phi[ROWS:TABLE, 0:F], f1, 0)
+    spread_ghosts(pfv_s, lambda: phi[ROWS:TABLE, F : 2 * F], f1, F)
 
     scale = 1.0 / math.sqrt(nbr.shape[0])
 
@@ -312,66 +352,76 @@
             planes += [(vel[j] - unit[j] * rate) * inv for j in range(3)]
             for number, value in enumerate(planes):
                 geo[side, number, rows, :] = value
+            for number, (a, s, c) in enumerate(WAVES[side](s1, c1)):
+                waves[0, side * NR + number, rows, :] = s
+                waves[1, side * NR + number, rows, :] = a * c
         return carry
 
     lax.fori_loop(0, ROWS // 8, geometry, 0)
 
-    def spread_table(refs, table, filters, at):
-        def body(p, carry):
-            for half in range(2):
-                weights = filters[pl.ds(2 * p + half, 1), at : at + F]
-                start = pl.multiple_of(p * SPAN + half * ROWS, ROWS)
-                hi, lo = split(table(0, ROWS) * weights)
-                refs[0, pl.ds(start, ROWS), :] = hi
-                refs[1, pl.ds(start, ROWS), :] = lo
-                start = pl.multiple_of(p * SPAN + 2 * ROWS + half * GHOSTS, GHOSTS)
-                hi, lo = split(table(ROWS, GHOSTS) * weights)
-                refs[0, pl.ds(start, GHOSTS), :] = hi
-                refs[1, pl.ds(start, GHOSTS), :] = lo
-            return carry
-
-        lax.fori_loop(0, PAIRS, body, 0)
-
-    spread_table(pfs_s, lambda at, n: phi[at : at + n, 0:F], f1, 0)
-    spread_table(pfv_s, lambda at, n: phi[at : at + n, F : 2 * F], f1, F)
-
-    def pair_rows(i, carry):
-        start = pl.multiple_of(i * 16, 16)
-        rows = pl.ds(start, 16)
-        for side in range(2):
-            g = [geo[side, number, rows, :] for number in range(13)]
-            e1d, e0d = g[E1] * g[DD], g[E0] * g[DD]
-            for at, a, s, c in WAVES[side](g[S1], g[C1]):
-                cols = slice(at, at + ROWS)
-                b = g[E0] * s
-                bd = e1d * s + e0d * (a * c)
-                put(lb, b, rows, cols)
-                put(lb, bd, pl.ds(start + ROWS, 16), cols)
-                for j in range(3):
-                    put(lv, b * g[U0 + j], pl.ds(start + j * ROWS, 16), cols)
-                    put(
-                        lv,
-                        bd * g[U0 + j] + b * g[W0 + j],
-                        pl.ds(start + (3 + j) * ROWS, 16),
-                        cols,
-                    )
+    lv = (lv0, lv1)
+
+    def build_pairs(m, target):
+        side = jnp.where(m < PAIRS, 0, 1)
+        cols = pl.ds(pl.multiple_of(m * TILE, TILE), TILE)
+        for start in range(0, ROWS, 16):
+            rows = slice(start, start + 16)
+
+            def twice(x):
+                return jnp.concatenate([x, x], 1)
+
+            e0, e1, rate = (geo[side, number, rows, :] for number in (E0, E1, DD))
+            e1d, e0d = twice(e1 * rate), twice(e0 * rate)
+            s = jnp.concatenate([waves[0, 2 * m + half, rows, :] for half in range(2)], 1)
+            ac = jnp.concatenate([waves[1, 2 * m + half, rows, :] for half in range(2)], 1)
+            b = twice(e0) * s
+            bd = e1d * s + e0d * ac
+            put_rows(lb, bd, start, start + 3 * ROWS, cols)
+            put_rows(lb, b, start + ROWS, start + 2 * ROWS, cols)
+            for j in range(3):
+                u, w = twice(geo[side, U0 + j, rows, :]), twice(geo[side, W0 + j, rows, :])
+                first = start + j * ROWS
+                put_rows(target, b * u, first, first + 6 * ROWS, slice(None))
+                first += 3 * ROWS
+                put_rows(target, bd * u + b * w, first, first + 6 * ROWS, slice(None))
+
+    def add_to(ref, rows, value, i):
+        if i == 0:
+            ref[rows, :] = value
+        else:
+            ref[rows, :] += value
+
+    def gather_scalar(refs, cols):
+        both = mm(lb[:, cols], refs[0, cols, :])
+        rest = mm(lb[0 : 2 * ROWS, cols], refs[1, cols, :])
+        acc[0:ROWS, :] += both[ROWS : 2 * ROWS] + both[2 * ROWS : 3 * ROWS] + rest[ROWS:]
+        acc[ROWS : 2 * ROWS, :] += both[0:ROWS] + both[3 * ROWS :] + rest[0:ROWS]
+
+    def gather_vector(m, near):
+        cols = pl.ds(pl.multiple_of(m * TILE, TILE), TILE)
+        both = mm(near[...], pfv_s[0, cols, :])
+        rest = mm(near[0 : 6 * ROWS, :], pfv_s[1, cols, :])
+        accv[...] += both[0 : 6 * ROWS] + both[6 * ROWS :] + rest
+
+    acc[...] = jnp.zeros((2 * ROWS, F), f32)
+    accv[...] = jnp.zeros((6 * ROWS, F), f32)
+    build_pairs(0, lv0)
+
+    def two_tiles(k, carry):
+        for half in range(2):
+            gather_vector(2 * k + half, lv[half])
+            build_pairs(2 * k + half + 1, lv[1 - half])
         return carry
 
-    lax.fori_loop(0, ROWS // 16, pair_rows, 0)
-
-    def gather_messages(target, left, rows, right):
-        def body(i, carry):
-            cols = pl.ds(pl.multiple_of(i * STEP, STEP), STEP)
-            b = right[0, cols, :], right[1, cols, :]
-            target[0:rows, :] += mm3((left[0][0:rows, cols], left[1][0:rows, cols]), b)
-            return carry
-
-        target[0:rows, :] = jnp.zeros((rows, F), f32)
-        lax.fori_loop(0, STEPS, body, 0)
-
-    gather_messages(acc, lv, 6 * ROWS, pfv_s)
-    lr[...] = mm3(split(acc[...]), (wlr_s[0], wlr_s[1]))
-    gather_messages(acc, lb, 2 * ROWS, pfs_s)
+    lax.fori_loop(0, TILES // 2, two_tiles, 0)
+    gather_vector(TILES - 1, lv0)
+
+    def scalar_step(i, carry):
+        gather_scalar(pfs_s, pl.ds(pl.multiple_of(i * STEP, STEP), STEP))
+        return carry
+
+    lax.fori_loop(0, STEPS, scalar_step, 0)
+    lr[...] = mm3(split(accv[...]), (wlr_s[0], wlr_s[1]))
 
     def part(j, side):
         return lr[j * ROWS : (j + 1) * ROWS, side * F : (side + 1) * F]
@@ -415,32 +465,45 @@
         def body(i, carry):
             start = pl.multiple_of(i * 16, 16)
             g = [pg[side, number, pl.ds(start, 16), :] for number in range(5)]
-            for q, (at, a, s, c) in enumerate(own_waves(g[3], g[4])):
-                cols = slice(q * ROWS, (q + 1) * ROWS)
-                put(lt, g[0] * s, pl.ds(start + side * ROWS, 16), cols)
-                put(
-                    lt,
-                    g[1] * s + g[2] * (a * c),
-                    pl.ds(start + side * ROWS + TABLE, 16),
-                    cols,
-                )
+            held = None
+            for q, (a, s, c) in enumerate(own_waves(g[3], g[4])):
+                new = (g[0] * s, g[1] * s + g[2] * (a * c))
+                if q % 2 == 0:
+                    held = new
+                    continue
+                cols = slice((q - 1) * ROWS, (q + 1) * ROWS)
+                for value, first, second in ((1, 0, 3), (0, 1, 2)):
+                    hi, lo = split(jnp.concatenate([held[value], new[value]], 1))
+                    lt[pl.ds(start + side * ROWS + first * TABLE, 16), cols] = hi
+                    lt[pl.ds(start + side * ROWS + second * TABLE, 16), cols] = lo
             return carry
 
         lax.fori_loop(0, count // 16, body, 0)
 
     turned(0, ROWS)
     turned(1, GHOSTS)
+
+    spread_own(p2_s, lambda: phi2[0, 0:ROWS, :], f2, 0)
+    spread_own(p2d_s, lambda: phi2[1, 0:ROWS, :], f2, 0)
 
     for copy in second:
         copy.wait()
     table_two(gnode[:, 0:F], gnode[:, F : 2 * F], ROWS, GHOSTS)
-    spread_table(p2_s, lambda at, n: phi2[0, at : at + n, :], f2, 0)
-    spread_table(p2d_s, lambda at, n: phi2[1, at : at + n, :], f2, 0)
-    gather_messages(acc, lb, 2 * ROWS, p2_s)
+    spread_ghosts(p2_s, lambda: phi2[0, ROWS:TABLE, :], f2, 0)
+    spread_ghosts(p2d_s, lambda: phi2[1, ROWS:TABLE, :], f2, 0)
+    acc[...] = jnp.zeros((2 * ROWS, F), f32)
+
+    def messages_two(i, carry):
+        cols = pl.ds(pl.multiple_of(i * STEP, STEP), STEP)
+        gather_scalar(p2_s, cols)
+        both = mm(lb[ROWS : 3 * ROWS, cols], p2d_s[0, cols, :])
+        rest = mm(lb[ROWS : 2 * ROWS, cols], p2d_s[1, cols, :])
+        acc[ROWS : 2 * ROWS, :] += both[0:ROWS] + both[ROWS:] + rest
+        return carry
+
+    lax.fori_loop(0, STEPS, messages_two, 0)
     st = node[:, 0:F] + acc[0:ROWS, :]
     std = node[:, F : 2 * F] + acc[ROWS : 2 * ROWS, :]
-    gather_messages(acc, lb, ROWS, p2d_s)
-    std = std + acc[0:ROWS, :]
 
     whs = wh_s[0], wh_s[1]
     v = mm3(split(st), whs)
@@ -453,25 +516,43 @@
         split(top * (sig * (1.0 - sig) * (2.0 + v * (1.0 - 2.0 * sig))) * vd), whs, NT
     )
 
-    for q in range(NR):
-        weights = f2[q : q + 1, :]
-        rows = slice(q % 4 * ROWS, (q % 4 + 1) * ROWS)
-        for number in range(2):
-            at = (number * NR // 4 + q // 4) * F
-            put(lv, mu[number] * weights, rows, slice(at, at + F))
-    bar[...] = jnp.zeros((2 * TABLE, F), f32)
-
-    def turned_messages(i, carry):
-        cols = pl.ds(pl.multiple_of(i * 512, 512), 512)
-        place = pl.ds(pl.multiple_of(i * F, F), F)
-        b = lvh[0 : 4 * ROWS, place], lvl[0 : 4 * ROWS, place]
-        bar[...] += mm3((lth[:, cols], ltl[:, cols]), b)
-        place = pl.ds(pl.multiple_of((NR // 4 + i) * F, F), F)
-        b = lvh[0 : 4 * ROWS, place], lvl[0 : 4 * ROWS, place]
-        bar[TABLE : 2 * TABLE, :] += mm3((lth[0:TABLE, cols], ltl[0:TABLE, cols]), b)
-        return carry
-
-    lax.fori_loop(0, NR * ROWS // 512, turned_messages, 0)
+    muf = (muf0, muf1)
+
+    def scaled(i):
+        for q in range(4 * i, 4 * i + 4):
+            weights = f2[q : q + 1, :]
+            rows = slice(q % 4 * ROWS, (q % 4 + 1) * ROWS)
+            for number in range(2):
+                hi, lo = split(mu[number] * weights)
+                muf[i % 2][2 * number, rows, :] = hi
+                muf[i % 2][2 * number + 1, rows, :] = lo
+
+    def turned_messages(i):
+        cols = slice(i * 4 * ROWS, (i + 1) * 4 * ROWS)
+        right = muf[i % 2]
+        both = mm(lt[:, cols], right[0])
+        rest = mm(lt[0 : 2 * TABLE, cols], right[1])
+        also = mm(lt[TABLE : 3 * TABLE, cols], right[2])
+        more = mm(lt[TABLE : 2 * TABLE, cols], right[3])
+        add_to(
+            bar,
+            slice(0, TABLE),
+            both[TABLE : 2 * TABLE] + both[2 * TABLE : 3 * TABLE] + rest[TABLE:],
+            i,
+        )
+        add_to(
+            bar,
+            slice(TABLE, 2 * TABLE),
+            (both[0:TABLE] + both[3 * TABLE :] + rest[0:TABLE])
+            + (also[0:TABLE] + also[TABLE:] + more),
+            i,
+        )
+
+    for i in range(NR // 4 + 1):
+        if i < NR // 4:
+            scaled(i)
+        if i > 0:
+            turned_messages(i - 1)
     back = mm3(split(bar[...]), w2[1], NT)
     v, vd = pre2[0], pre2[1]
     sig = sigmoid(v)
@@ -488,13 +569,20 @@
 
     m = split(mu[0])
     md = split(mu[1])
+    high = jnp.concatenate([m[0], md[0]], 0)
+    full = jnp.concatenate([high, m[1], md[1]], 0)
+    ours = jnp.concatenate(m, 0)
 
     def pairs_two(i, carry):
         cols = pl.ds(pl.multiple_of(i * STEP, STEP), STEP)
-        b = p2_s[0, cols, :], p2_s[1, cols, :]
-        bd = p2d_s[0, cols, :], p2d_s[1, cols, :]
-        out[0:ROWS, cols] = mm3(m, b, NT)
-        out[ROWS : 2 * ROWS, cols] = mm3(md, b, NT) + mm3(m, bd, NT)
+        both = mm(full, p2_s[0, cols, :], NT)
+        rest = mm(high, p2_s[1, cols, :], NT)
+        also = mm(ours, p2d_s[0, cols, :], NT)
+        more = mm(m[0], p2d_s[1, cols, :], NT)
+        two[0:ROWS, cols] = both[0:ROWS] + both[2 * ROWS : 3 * ROWS] + rest[0:ROWS]
+        two[ROWS : 2 * ROWS, cols] = (
+            both[ROWS : 2 * ROWS] + both[3 * ROWS :] + rest[ROWS:]
+        ) + (also[0:ROWS] + also[ROWS:] + more)
         return carry
 
     lax.fori_loop(0, STEPS, pairs_two, 0)
@@ -517,60 +605,97 @@
         lr[j * ROWS : (j + 1) * ROWS, F : 2 * F] = nu * l
         lr[(3 + j) * ROWS : (4 + j) * ROWS, 0:F] = nud * r + nu * rd
         lr[(3 + j) * ROWS : (4 + j) * ROWS, F : 2 * F] = nud * l + nu * ld
-    acc[...] = mm3(split(lr[...]), wlr, NT)
-    n = split(jnp.concatenate([mu[0], mu[1]], 0))
-    vb = split(acc[...])
-    lvb = lv[0].at[:, 0:F], lv[1].at[:, 0:F]
-    lvb[0][...] = vb[0]
-    lvb[1][...] = vb[1]
-
-    def pairs_one(i, carry):
-        cols = pl.ds(pl.multiple_of(i * STEP, STEP), STEP)
-        out[0 : 2 * ROWS, cols] += mm3(n, (pfs_s[0, cols, :], pfs_s[1, cols, :]), NT)
-        out[2 * ROWS :, cols] = mm3(
-            (lvb[0][...], lvb[1][...]), (pfv_s[0, cols, :], pfv_s[1, cols, :]), NT
-        )
+    hi, lo = split(mm3(split(lr[...]), wlr, NT))
+    vbar[0 : 6 * ROWS, :] = hi
+    vbar[6 * ROWS :, :] = lo
+    for number in range(2):
+        hi, lo = split(mu[number])
+        nus[number * ROWS : (number + 1) * ROWS, :] = hi
+        nus[(2 + number) * ROWS : (3 + number) * ROWS, :] = lo
+    out = (out0, out1)
+
+    def pairs_one(m, target):
+        cols = pl.ds(pl.multiple_of(m * TILE, TILE), TILE)
+        both = mm(nus[...], pfs_s[0, cols, :], NT)
+        rest = mm(nus[0 : 2 * ROWS, :], pfs_s[1, cols, :], NT)
+        target[0 : 2 * ROWS, :] = two[:, cols] + (both[0 : 2 * ROWS] + both[2 * ROWS :] + rest)
+        both = mm(vbar[...], pfv_s[0, cols, :], NT)
+        rest = mm(vbar[0 : 6 * ROWS, :], pfv_s[1, cols, :], NT)
+        target[2 * ROWS :, :] = both[0 : 6 * ROWS] + both[6 * ROWS :] + rest
+
+    upper = lax.broadcasted_iota(jnp.int32, (8, ROWS), 1) >= GHOSTS
+
+    def sum_waves(m, source):
+        side = jnp.where(m < PAIRS, 0, 1)
+        base = jnp.where(m < PAIRS, 2 * m + 1, 4 * (m - PAIRS) + 1).astype(f32)
+        jump = jnp.where(m < PAIRS, 1.0, 2.0)
+        ghosts_on = jnp.where(m < PAIRS, 0.0, 1.0)
+        a = [
+            KAPPA * (base + half * jump + ghosts_on * jnp.where(upper, 1.0, 0.0))
+            for half in range(2)
+        ]
+        aa = [x * x for x in a]
+        for start in range(0, ROWS, 8):
+            rows = slice(start, start + 8)
+            u = [geo[side, U0 + j, rows, :] for j in range(3)]
+            total = [sums[side, number, rows, :] for number in range(14)]
+            for half in range(2):
+                s = waves[0, 2 * m + half, rows, :]
+                ac = waves[1, 2 * m + half, rows, :]
+                ss = s * aa[half]
+                cols = slice(half * ROWS, (half + 1) * ROWS)
+                y = [source[start + k * ROWS : start + k * ROWS + 8, cols] for k in range(8)]
+                along = y[0] + u[0] * y[2] + u[1] * y[3] + u[2] * y[4]
+                along_d = y[1] + u[0] * y[5] + u[1] * y[6] + u[2] * y[7]
+                for j in range(3):
+                    total[j] += s * y[2 + j]
+                    total[3 + j] += ac * y[2 + j]
+                    total[6 + j] += s * y[5 + j]
+                total[9] += s * y[0]
+                total[10] += ac * y[0]
+                total[11] += ss * along
+                total[12] += s * y[1]
+                total[13] += ac * along_d
+            for number in range(14):
+                sums[side, number, rows, :] = total[number]
+
+    sums[...] = jnp.zeros(sums.shape, f32)
+    pairs_one(0, out0)
+
+    def two_sums(k, carry):
+        for half in range(2):
+            pairs_one(2 * k + half + 1, out[1 - half])
+            sum_waves(2 * k + half, out[half])
         return carry
 
-    lax.fori_loop(0, STEPS, pairs_one, 0)
+    lax.fori_loop(0, TILES // 2, two_sums, 0)
+    sum_waves(TILES - 1, out0)
 
     def offsets_back(i, carry):
-        start = pl.multiple_of(i * 8, 8)
-        rows = pl.ds(start, 8)
+        rows = pl.ds(pl.multiple_of(i * 8, 8), 8)
         for side in range(2):
-            zero = jnp.zeros((8, ROWS), f32)
-            z = [[zero] * 4 for _ in range(3)]
-            zd = [[zero] * 4 for _ in range(2)]
-            for at, a, s, c in WAVES[side](geo[side, S1, rows, :], geo[side, C1, rows, :]):
-                cols = slice(at, at + ROWS)
-                ac = a * c
-                aas = a * (a * s)
-                for k in range(4):
-                    y = out[pl.ds(start + (0 if k == 3 else 2 + k) * ROWS, 8), cols]
-                    yd = out[pl.ds(start + (1 if k == 3 else 5 + k) * ROWS, 8), cols]
-                    z[0][k] = z[0][k] + s * y
-                    z[1][k] = z[1][k] + ac * y
-                    z[2][k] = z[2][k] + aas * y
-                    zd[0][k] = zd[0][k] + s * yd
-                    zd[1][k] = zd[1][k] + ac * yd
             e0, e1, e2, rate, inv = (geo[side, number, rows, :] for number in range(5))
             unit = [geo[side, U0 + j, rows, :] for j in range(3)]
             turn = [geo[side, W0 + j, rows, :] for j in range(3)]
-            a_, ad, ub, ubd = [], [], [], []
-            for k in range(4):
-                first_d = e1 * z[0][k] + e0 * z[1][k]
-                second_d = e2 * z[0][k] + 2.0 * e1 * z[1][k] - e0 * z[2][k]
-                a_.append(first_d)
-                ad.append(rate * second_d + e1 * zd[0][k] + e0 * zd[1][k])
-                if k < 3:
-                    ub.append(e0 * z[0][k])
-                    ubd.append(rate * first_d + e0 * zd[0][k])
-            db, dbd, w, wd = a_[3], ad[3], zero, zero
+            z = [sums[side, number, rows, :] for number in range(14)]
+            db = e1 * z[9] + e0 * z[10]
+            dbd = e2 * z[9] + 2.0 * e1 * z[10] - e0 * z[11]
+            inner = z[12]
+            w = jnp.zeros((8, ROWS), f32)
+            wd = w
+            spin = w
+            ub, ubd = [], []
             for j in range(3):
-                db = db + unit[j] * a_[j]
-                dbd = dbd + turn[j] * a_[j] + unit[j] * ad[j]
+                slope = e1 * z[j] + e0 * z[3 + j]
+                ub.append(e0 * z[j])
+                ubd.append(rate * slope + e0 * z[6 + j])
+                db = db + unit[j] * slope
+                dbd = dbd + unit[j] * (e2 * z[j] + 2.0 * e1 * z[3 + j])
+                inner = inner + unit[j] * z[6 + j]
+                spin = spin + turn[j] * slope
                 w = w + unit[j] * ub[j]
                 wd = wd + turn[j] * ub[j] + unit[j] * ubd[j]
+            dbd = rate * dbd + e1 * inner + e0 * z[13] + spin
             for j in range(3):
                 t = (ub[j] - unit[j] * w) * inv
                 pg[side, j, rows, :] = db * unit[j] + t
@@ -644,17 +769,19 @@
         v32(2, ROWS, ROWS),
         v32(6, ROWS, ROWS),
         v32(2, 13, ROWS, ROWS),
-        v16(2 * ROWS, WIDE),
-        v16(2 * ROWS, WIDE),
-        v16(6 * ROWS, WIDE),
-        v16(6 * ROWS, WIDE),
-        v16(2 * TABLE, NR * ROWS),
-        v16(2 * TABLE, NR * ROWS),
+        v32(2, NR + PAIRS, ROWS, ROWS),
+        v16(4 * ROWS, WIDE),
+        v16(12 * ROWS, TILE),
+        v16(12 * ROWS, TILE),
+        v16(4 * TABLE, NR * ROWS),
         v16(2, WIDE, F),
         v16(2, WIDE, F),
         v16(2, WIDE, F),
         v16(2, WIDE, F),
+        v16(4, 4 * ROWS, F),
+        v16(4, 4 * ROWS, F),
         v32(TABLE, 2 * F),
+        v32(2 * ROWS, F),
         v32(6 * ROWS, F),
         v32(6 * ROWS, 2 * F),
         v32(ROWS, 2 * F),
@@ -662,7 +789,13 @@
         v32(2, TABLE, F),
         v32(2, ROWS, F),
         v32(2 * TABLE, F),
-        v32(8 * ROWS, WIDE),
+        v32(8 * ROWS, TILE),
+        v32(8 * ROWS, TILE),
+        v32(3 * F, 3 * F),
+        v32(2 * ROWS, WIDE),
+        v32(2, 14, ROWS, ROWS),
+        v16(12 * ROWS, F),
+        v16(4 * ROWS, F),
         v32(2, 6, ROWS, ROWS),
     ] + [dma] * 11
     out = jax.ShapeDtypeStruct((3, ROWS), f32)

time: 75.7 us -> 67.7 us (0.89)
  Pallas kernels: 72.3 us -> 64.4 us
    pallas_call x1, Pallas kernels: 72.3 us -> 64.4 us  [per_device(): pl.pallas_call(functools.partial(kernel, nx, ny), out_shape=(out, out), i...]
where the time goes in v2:
time: 67.7 us; the launch traced here: 67.6 us
  Pallas kernels  64.4 us (95%)
  local copies, waits for them, and re-layouts  1.89 us (3%)
  between operations  1.3 us (2%)
    pallas_call x1, Pallas kernels, per_device(): pl.pallas_call(functools.partial(kernel, nx, ny), out_shape=(out, out), i...  64.4 us
    unnamed x6, local copies, waits for them, and re-layouts  1.89 us

profile of v2, /device:TPU:0, one launch (start us, length us, event | category | flops | bytes accessed | tf_op | source)
XLA Modules:
  0.0 67.6 jit_solution(15969975281823914457)
XLA Ops:
  1.3 64.4 %shard_map.167 = (f32[3,128]{1,0:T(4,128)}, f32[3,128]{1,0:T(4,128)}) custom-call(f32[3,128]{1,0:T(4,128)} %pos.1, f32[3,128]{1,0:T(4,128)} %tan.1, f32[128,256]{1,0:T(8,128)} %emb.1, s32[1]{0:T(128)S(6)} %copy.20.cnt, s32[32,128]{1,0:T(8,128)} %nbr.1, s32[1,64]{1,0:T(1,128)} %snd.1, f32[256,256]{1,0:T(8,128)} %w1i.1, f32[256,512]{1,0:T(8,128)} %w1o.1, ...), custom_call_target="tpu_custom_call" | custom-call | tf_op jit(solution)/shard_map/pallas_call | solution.py:802
  65.7 0.0 copy-start.1
  65.7 0.7 copy-done.1
  66.3 0.0 copy-start
  66.3 0.6 copy.21
  66.9 0.1 copy-done
  67.0 0.6 copy.22
Async XLA Ops:
  65.7 0.7 copy-start.1
  66.3 0.7 copy-start

commit v3 on v2

--- a/solution.py
+++ b/solution.py
@@ -109,24 +109,32 @@
 def kernel(
     nx,
     ny,
-    pos,
-    tan,
-    emb,
+    pos_in,
+    tan_in,
+    emb_in,
     cnt,
-    nbr,
-    snd,
+    nbr_in,
+    snd_in,
     w1i,
     w1o,
-    f1,
+    f1_in,
     wl,
     wr,
     w2i,
     w2o,
-    f2,
+    f2_in,
     wh,
-    we,
+    we_in,
     force,
     hess,
+    pos,
+    tan,
+    emb,
+    nbr,
+    snd,
+    f1,
+    f2,
+    we,
     w1i_s,
     w1o_s,
     wlr_s,
@@ -234,8 +242,16 @@
     for number, (w, (down, at)) in enumerate(zip((w1i, w1o, wl, wr, w2i, w2o, wh), spots)):
         place = landing.at[down * F : (down + 1) * F, at : at + w.shape[1]]
         weights.append((pltpu.make_async_copy(w, place, loads.at[number]), place))
+    small = {}
+    named = ((snd_in, snd), (pos_in, pos), (tan_in, tan), (emb_in, emb), (nbr_in, nbr))
+    named += ((f1_in, f1), (f2_in, f2), (we_in, we))
+    for number, (source, place) in enumerate(named):
+        small[number] = pltpu.make_async_copy(source, place, loads.at[7 + number])
+        small[number].start()
     for copy, _ in weights:
         copy.start()
+    for number in range(4):
+        small[number].wait()
 
     sndpad[...] = jnp.full((8, ROWS), -1, jnp.int32)
     sndpad[0:1, 0:GHOSTS] = snd[...]
@@ -251,12 +267,6 @@
     hot16 = hot.astype(bf16)
     csel[...] = mm(hi, hot16) + (mm(mid, hot16) + mm(lo, hot16))
     sel1[...] = select(emb[...])
-    pl.semaphore_wait(barrier, 8)
-    coords = copies(csel, crecv, sendc, recvc, 1, True)
-    first = copies(sel1, gemb, send1, recv1, 1, False)
-    for copy in coords + first:
-        copy.start()
-
     stores = ((w1i_s, 0), (w1o_s, 0), (wlr_s, 0), (wlr_s, F), (w2i_s, 0), (w2o_s, 0), (wh_s, 0))
     for (refs, at), (copy, place) in zip(stores, weights):
         copy.wait()
@@ -264,6 +274,7 @@
         refs[0, :, at : at + hi.shape[1]] = hi
         refs[1, :, at : at + hi.shape[1]] = lo
 
+    small[4].wait()
     row = lax.broadcasted_iota(jnp.int32, (ROWS, ROWS), 0)
     ghost = lax.rem(row, GHOSTS)
     for side, slots in ((0, row), (1, ROWS + (7 - lax.div(ghost, 8)) * 8 + lax.rem(ghost, 8))):
@@ -273,6 +284,9 @@
 
         listed = lax.fori_loop(0, nbr.shape[0], mark, jnp.zeros((ROWS, ROWS), f32))
         mask[side] = listed.T
+
+    for number in (5, 6, 7):
+        small[number].wait()
 
     def project(rows, first_w, second_w):
         v = mm3(split(rows), first_w)
@@ -312,52 +326,38 @@
     spread_own(pfs_s, lambda: phi[0:ROWS, 0:F], f1, 0)
     spread_own(pfv_s, lambda: phi[0:ROWS, F : 2 * F], f1, F)
 
-    for copy in coords + first:
-        copy.wait()
-    phi[ROWS:TABLE, :] = project(gemb[...], *w1)
-    found = merged(crecv)
-    twofold = found + pltpu.roll(found, GHOSTS, 1)
-    csel2 = (c8[...], twofold)
-
-    spread_ghosts(pfs_s, lambda: phi[ROWS:TABLE, 0:F], f1, 0)
-    spread_ghosts(pfv_s, lambda: phi[ROWS:TABLE, F : 2 * F], f1, F)
-
     scale = 1.0 / math.sqrt(nbr.shape[0])
 
-    def geometry(i, carry):
+    def geometry(i, carry, side, table):
         rows = pl.ds(pl.multiple_of(i * 8, 8), 8)
         centre = [colb[j, rows, :] for j in range(6)]
-        for side in range(2):
-            table = csel2[side]
-            off = [table[j : j + 1, :] - centre[j] for j in range(3)]
-            vel = [table[j : j + 1, :] - centre[j] for j in range(3, 6)]
-            listed = mask[side, rows, :]
-            sq = off[0] * off[0] + off[1] * off[1] + off[2] * off[2]
-            sq = jnp.where(listed > 0.0, sq, 1.0) + SOFT
-            inv = lax.rsqrt(sq)
-            inv = inv * (1.5 - 0.5 * sq * inv * inv)
-            dist = sq * inv
-            unit = [x * inv for x in off]
-            rate = unit[0] * vel[0] + unit[1] * vel[1] + unit[2] * vel[2]
-            s1, c1 = sin_cos(KAPPA * dist)
-            weight = scale * listed
-            env = 0.5 * (c1 + 1.0)
-            env1 = (-0.5 * KAPPA) * s1
-            env2 = (-0.5 * KAPPA * KAPPA) * c1
-            e0 = weight * env * inv
-            slope = env1 - env * inv
-            e1 = weight * inv * slope
-            e2 = weight * inv * (env2 - 2.0 * inv * slope)
-            planes = [e0, e1, e2, rate, inv, s1, c1] + unit
-            planes += [(vel[j] - unit[j] * rate) * inv for j in range(3)]
-            for number, value in enumerate(planes):
-                geo[side, number, rows, :] = value
-            for number, (a, s, c) in enumerate(WAVES[side](s1, c1)):
-                waves[0, side * NR + number, rows, :] = s
-                waves[1, side * NR + number, rows, :] = a * c
+        off = [table[j : j + 1, :] - centre[j] for j in range(3)]
+        vel = [table[j : j + 1, :] - centre[j] for j in range(3, 6)]
+        listed = mask[side, rows, :]
+        sq = off[0] * off[0] + off[1] * off[1] + off[2] * off[2]
+        sq = jnp.where(listed > 0.0, sq, 1.0) + SOFT
+        inv = lax.rsqrt(sq)
+        inv = inv * (1.5 - 0.5 * sq * inv * inv)
+        dist = sq * inv
+        unit = [x * inv for x in off]
+        rate = unit[0] * vel[0] + unit[1] * vel[1] + unit[2] * vel[2]
+        s1, c1 = sin_cos(KAPPA * dist)
+        weight = scale * listed
+        env = 0.5 * (c1 + 1.0)
+        env1 = (-0.5 * KAPPA) * s1
+        env2 = (-0.5 * KAPPA * KAPPA) * c1
+        e0 = weight * env * inv
+        slope = env1 - env * inv
+        e1 = weight * inv * slope
+        e2 = weight * inv * (env2 - 2.0 * inv * slope)
+        planes = [e0, e1, e2, rate, inv, s1, c1] + unit
+        planes += [(vel[j] - unit[j] * rate) * inv for j in range(3)]
+        for number, value in enumerate(planes):
+            geo[side, number, rows, :] = value
+        for number, (a, s, c) in enumerate(WAVES[side](s1, c1)):
+            waves[0, side * NR + number, rows, :] = s
+            waves[1, side * NR + number, rows, :] = a * c
         return carry
-
-    lax.fori_loop(0, ROWS // 8, geometry, 0)
 
     lv = (lv0, lv1)
 
@@ -403,18 +403,41 @@
         rest = mm(near[0 : 6 * ROWS, :], pfv_s[1, cols, :])
         accv[...] += both[0 : 6 * ROWS] + both[6 * ROWS :] + rest
 
+    lax.fori_loop(0, ROWS // 8, functools.partial(geometry, side=0, table=c8[...]), 0)
+    build_pairs(0, lv0)
+    pl.semaphore_wait(barrier, 8)
+    coords = copies(csel, crecv, sendc, recvc, 1, True)
+    first = copies(sel1, gemb, send1, recv1, 1, False)
+    for copy in coords + first:
+        copy.start()
+
     acc[...] = jnp.zeros((2 * ROWS, F), f32)
     accv[...] = jnp.zeros((6 * ROWS, F), f32)
-    build_pairs(0, lv0)
-
-    def two_tiles(k, carry):
+
+    def two_tiles(k, carry, base, last):
         for half in range(2):
-            gather_vector(2 * k + half, lv[half])
-            build_pairs(2 * k + half + 1, lv[1 - half])
+            m = base + 2 * k + half
+            gather_vector(m, lv[half])
+            build_pairs(jnp.minimum(m + 1, last), lv[1 - half])
         return carry
 
-    lax.fori_loop(0, TILES // 2, two_tiles, 0)
+    lax.fori_loop(0, PAIRS // 2, functools.partial(two_tiles, base=0, last=PAIRS - 1), 0)
+
+    for copy in coords + first:
+        copy.wait()
+    phi[ROWS:TABLE, :] = project(gemb[...], *w1)
+    found = merged(crecv)
+    twofold = found + pltpu.roll(found, GHOSTS, 1)
+    lax.fori_loop(0, ROWS // 8, functools.partial(geometry, side=1, table=twofold), 0)
+    build_pairs(PAIRS, lv0)
+
+    spread_ghosts(pfs_s, lambda: phi[ROWS:TABLE, 0:F], f1, 0)
+    spread_ghosts(pfv_s, lambda: phi[ROWS:TABLE, F : 2 * F], f1, F)
+    lax.fori_loop(
+        0, (TILES - PAIRS) // 2, functools.partial(two_tiles, base=PAIRS, last=TILES - 1), 0
+    )
     gather_vector(TILES - 1, lv0)
+
 
     def scalar_step(i, carry):
         gather_scalar(pfs_s, pl.ds(pl.multiple_of(i * STEP, STEP), STEP))
@@ -660,67 +683,82 @@
                 sums[side, number, rows, :] = total[number]
 
     sums[...] = jnp.zeros(sums.shape, f32)
-    pairs_one(0, out0)
-
-    def two_sums(k, carry):
+    pairs_one(PAIRS, out0)
+
+    def two_sums(k, carry, first, second, base, last):
         for half in range(2):
-            pairs_one(2 * k + half + 1, out[1 - half])
-            sum_waves(2 * k + half, out[half])
+            ahead, behind = (first, second) if half == 0 else (second, first)
+            m = base + 2 * k + half
+            pairs_one(jnp.minimum(m + 1, last), ahead)
+            sum_waves(m, behind)
         return carry
 
-    lax.fori_loop(0, TILES // 2, two_sums, 0)
+    lax.fori_loop(
+        0,
+        (TILES - PAIRS) // 2,
+        functools.partial(two_sums, first=out1, second=out0, base=PAIRS, last=TILES - 1),
+        0,
+    )
+    pairs_one(0, out1)
     sum_waves(TILES - 1, out0)
 
-    def offsets_back(i, carry):
+    def offsets_back(i, carry, side):
         rows = pl.ds(pl.multiple_of(i * 8, 8), 8)
-        for side in range(2):
-            e0, e1, e2, rate, inv = (geo[side, number, rows, :] for number in range(5))
-            unit = [geo[side, U0 + j, rows, :] for j in range(3)]
-            turn = [geo[side, W0 + j, rows, :] for j in range(3)]
-            z = [sums[side, number, rows, :] for number in range(14)]
-            db = e1 * z[9] + e0 * z[10]
-            dbd = e2 * z[9] + 2.0 * e1 * z[10] - e0 * z[11]
-            inner = z[12]
-            w = jnp.zeros((8, ROWS), f32)
-            wd = w
-            spin = w
-            ub, ubd = [], []
-            for j in range(3):
-                slope = e1 * z[j] + e0 * z[3 + j]
-                ub.append(e0 * z[j])
-                ubd.append(rate * slope + e0 * z[6 + j])
-                db = db + unit[j] * slope
-                dbd = dbd + unit[j] * (e2 * z[j] + 2.0 * e1 * z[3 + j])
-                inner = inner + unit[j] * z[6 + j]
-                spin = spin + turn[j] * slope
-                w = w + unit[j] * ub[j]
-                wd = wd + turn[j] * ub[j] + unit[j] * ubd[j]
-            dbd = rate * dbd + e1 * inner + e0 * z[13] + spin
-            for j in range(3):
-                t = (ub[j] - unit[j] * w) * inv
-                pg[side, j, rows, :] = db * unit[j] + t
-                pg[side, 3 + j, rows, :] = (
-                    dbd * unit[j]
-                    + db * turn[j]
-                    + (ubd[j] - turn[j] * w - unit[j] * wd - t * rate) * inv
-                )
+        e0, e1, e2, rate, inv = (geo[side, number, rows, :] for number in range(5))
+        unit = [geo[side, U0 + j, rows, :] for j in range(3)]
+        turn = [geo[side, W0 + j, rows, :] for j in range(3)]
+        z = [sums[side, number, rows, :] for number in range(14)]
+        db = e1 * z[9] + e0 * z[10]
+        dbd = e2 * z[9] + 2.0 * e1 * z[10] - e0 * z[11]
+        inner = z[12]
+        w = jnp.zeros((8, ROWS), f32)
+        wd = w
+        spin = w
+        ub, ubd = [], []
+        for j in range(3):
+            slope = e1 * z[j] + e0 * z[3 + j]
+            ub.append(e0 * z[j])
+            ubd.append(rate * slope + e0 * z[6 + j])
+            db = db + unit[j] * slope
+            dbd = dbd + unit[j] * (e2 * z[j] + 2.0 * e1 * z[3 + j])
+            inner = inner + unit[j] * z[6 + j]
+            spin = spin + turn[j] * slope
+            w = w + unit[j] * ub[j]
+            wd = wd + turn[j] * ub[j] + unit[j] * ubd[j]
+        dbd = rate * dbd + e1 * inner + e0 * z[13] + spin
+        for j in range(3):
+            t = (ub[j] - unit[j] * w) * inv
+            pg[side, j, rows, :] = db * unit[j] + t
+            pg[side, 3 + j, rows, :] = (
+                dbd * unit[j]
+                + db * turn[j]
+                + (ubd[j] - turn[j] * w - unit[j] * wd - t * rate) * inv
+            )
         return carry
 
-    lax.fori_loop(0, ROWS // 8, offsets_back, 0)
-
+    lax.fori_loop(0, ROWS // 8, functools.partial(offsets_back, side=1), 0)
     gpos[...] = jnp.zeros((8, ROWS), f32)
     c8[...] = jnp.zeros((8, ROWS), f32)
     for j in range(6):
         ghosts = pg[1, j]
-        own = pg[0, j]
-        halves = jnp.sum(ghosts, axis=0, keepdims=True)
-        gpos[j : j + 1, :] = halves
-        c8[j : j + 1, :] = jnp.sum(own - own.T - ghosts.T, axis=0, keepdims=True)
+        gpos[j : j + 1, :] = jnp.sum(ghosts, axis=0, keepdims=True)
+        c8[j : j + 1, :] = jnp.sum(ghosts.T, axis=0, keepdims=True)
     both = gpos[...]
     gpos[...] = both + pltpu.roll(both, GHOSTS, 1)
     last = copies(gpos, rpos, send4, recv4, -1, True)
     for copy in last:
         copy.start()
+
+    lax.fori_loop(
+        0,
+        PAIRS // 2,
+        functools.partial(two_sums, first=out0, second=out1, base=0, last=PAIRS - 1),
+        0,
+    )
+    lax.fori_loop(0, ROWS // 8, functools.partial(offsets_back, side=0), 0)
+    for j in range(6):
+        own = pg[0, j]
+        c8[j : j + 1, :] = jnp.sum(own - own.T, axis=0, keepdims=True) - c8[j : j + 1, :]
     for copy in last:
         copy.wait()
     hi, mid, lo = split3(merged(rpos))
@@ -734,10 +772,8 @@
     arrays = list(arrays)
     arrays[15] = arrays[15].reshape(1, F)
     vmem = pl.BlockSpec(memory_space=pltpu.VMEM)
-    in_specs = [vmem] * 16
+    in_specs = [pl.BlockSpec(memory_space=pl.ANY)] * 16
     in_specs[3] = pl.BlockSpec(memory_space=pltpu.SMEM)
-    for number in (6, 7, 9, 10, 11, 12, 14):
-        in_specs[number] = pl.BlockSpec(memory_space=pl.ANY)
 
     def v32(*shape):
         return pltpu.VMEM(shape, f32)
@@ -747,6 +783,14 @@
 
     dma = pltpu.SemaphoreType.DMA((8,))
     scratch = [
+        v32(3, ROWS),
+        v32(3, ROWS),
+        v32(ROWS, F),
+        pltpu.VMEM(arrays[4].shape, jnp.int32),
+        pltpu.VMEM((1, GHOSTS), jnp.int32),
+        v32(NR, 2 * F),
+        v32(NR, F),
+        v32(1, F),
         v16(2, F, F),
         v16(2, F, 2 * F),
         v16(2, F, 2 * F),
@@ -797,7 +841,7 @@
         v16(12 * ROWS, F),
         v16(4 * ROWS, F),
         v32(2, 6, ROWS, ROWS),
-    ] + [dma] * 11
+    ] + [dma] * 10 + [pltpu.SemaphoreType.DMA((15,))]
     out = jax.ShapeDtypeStruct((3, ROWS), f32)
     return pl.pallas_call(
         functools.partial(kernel, nx, ny),

time: 67.7 us -> 60.7 us (0.90)
  Pallas kernels: 64.4 us -> 57.3 us
    pallas_call x1, Pallas kernels: 64.4 us -> 57.3 us  [per_device(): pl.pallas_call(functools.partial(kernel, nx, ny), out_shape=(out, out), i...]
where the time goes in v3:
time: 60.7 us; the launch traced here: 60.5 us
  Pallas kernels  57.3 us (94%)
  local copies, waits for them, and re-layouts  1.89 us (3%)
  between operations  1.3 us (2%)
    pallas_call x1, Pallas kernels, per_device(): pl.pallas_call(functools.partial(kernel, nx, ny), out_shape=(out, out), i...  57.3 us
    unnamed x6, local copies, waits for them, and re-layouts  1.89 us

profile of v3, /device:TPU:0, one launch (start us, length us, event | category | flops | bytes accessed | tf_op | source)
XLA Modules:
  0.0 60.5 jit_solution(17554499975821608288)
XLA Ops:
  1.3 57.3 %shard_map.167 = (f32[3,128]{1,0:T(4,128)}, f32[3,128]{1,0:T(4,128)}) custom-call(f32[3,128]{1,0:T(4,128)} %pos_in.1, f32[3,128]{1,0:T(4,128)} %tan_in.1, f32[128,256]{1,0:T(8,128)} %emb_in.1, s32[1]{0:T(128)S(6)} %copy.20.cnt, s32[32,128]{1,0:T(8,128)} %nbr_in.1, s32[1,64]{1,0:T(1,128)} %snd_in.1, f32[256,256]{1,0:T(8,128)} %w1i.1, f32[256,512]{1,0:T(8,128)} %w1o.1, ...), custom_call_target="tpu_custom_call" | custom-call | tf_op jit(solution)/shard_map/pallas_call | solution.py:846
  58.6 0.0 copy-start.1
  58.6 0.7 %copy-done.1 = f32[3,128]{1,0:T(4,128)S(1)} copy-done((f32[3,128]{1,0:T(4,128)S(1)}, f32[3,128]{1,0:T(4,128)}, u32[]{:S(2)}) %copy-start.1) | copy-done | bytes 1560
  59.2 0.0 copy-start
  59.2 0.6 copy.21
  59.8 0.1 copy-done
  59.9 0.6 copy.22
Async XLA Ops:
  58.6 0.7 %copy-start.1 = (f32[3,128]{1,0:T(4,128)S(1)}, f32[3,128]{1,0:T(4,128)}, u32[]{:S(2)}) copy-start(f32[3,128]{1,0:T(4,128)} %get-tuple-element.4) | copy-start | bytes 4612
  59.2 0.7 %copy-start = (f32[3,128]{1,0:T(4,128)S(1)}, f32[3,128]{1,0:T(4,128)}, u32[]{:S(2)}) copy-start(f32[3,128]{1,0:T(4,128)} %get-tuple-element.5) | copy-start | bytes 4612

commit v4 on v3

--- a/solution.py
+++ b/solution.py
@@ -25,8 +25,8 @@
 TILE = 256
 TILES = NR * TABLE // TILE
 WIDE = TILES * TILE
-STEP = 3 * TILE
-STEPS = WIDE // STEP
+GROUP = 5
+GROUPS = NR // GROUP
 
 
 def split(x):
@@ -158,16 +158,14 @@
     colb,
     geo,
     waves,
-    lb,
+    bq,
     lv0,
     lv1,
     lt,
-    pfs_s,
     pfv_s,
-    p2_s,
-    p2d_s,
-    muf0,
-    muf1,
+    tab,
+    wmu,
+    scaled,
     phi,
     acc,
     accv,
@@ -183,7 +181,6 @@
     two,
     sums,
     vbar,
-    nus,
     pg,
     send1,
     recv1,
@@ -318,12 +315,23 @@
 
         lax.fori_loop(0, NR, body, 0)
 
-    def put_rows(ref, value, first, second, cols):
+    def put_rows(ref, value, first, second):
         hi, lo = split(value)
-        ref[first : first + 16, cols] = hi
-        ref[second : second + 16, cols] = lo
-
-    spread_own(pfs_s, lambda: phi[0:ROWS, 0:F], f1, 0)
+        ref[first : first + 16, :] = hi
+        ref[second : second + 16, :] = lo
+
+    def fill_own(number, value):
+        put2(tab.at[number], value, 0)
+
+    def fill_ghosts(number, value):
+        for start in (ROWS, TABLE):
+            put2(tab.at[number], value, start)
+
+    def place(q, rows):
+        i, k = (q // GROUP, q % GROUP) if isinstance(q, int) else (lax.div(q, GROUP), lax.rem(q, GROUP))
+        return 2 * GROUP * rows * i + rows * k
+
+    fill_own(0, phi[0:ROWS, 0:F])
     spread_own(pfv_s, lambda: phi[0:ROWS, F : 2 * F], f1, F)
 
     scale = 1.0 / math.sqrt(nbr.shape[0])
@@ -361,9 +369,8 @@
 
     lv = (lv0, lv1)
 
-    def build_pairs(m, target):
-        side = jnp.where(m < PAIRS, 0, 1)
-        cols = pl.ds(pl.multiple_of(m * TILE, TILE), TILE)
+    def build_pairs(m, target, side):
+        upper = lax.broadcasted_iota(jnp.int32, (16, ROWS), 1) >= GHOSTS
         for start in range(0, ROWS, 16):
             rows = slice(start, start + 16)
 
@@ -376,26 +383,39 @@
             ac = jnp.concatenate([waves[1, 2 * m + half, rows, :] for half in range(2)], 1)
             b = twice(e0) * s
             bd = e1d * s + e0d * ac
-            put_rows(lb, bd, start, start + 3 * ROWS, cols)
-            put_rows(lb, b, start + ROWS, start + 2 * ROWS, cols)
+            for number, value in enumerate((b, bd)):
+                for half in range(2):
+                    x = value[:, half * ROWS : (half + 1) * ROWS]
+                    if side == 0:
+                        found = ((2 * m + half, x),)
+                    else:
+                        q = 4 * (m - PAIRS) + 2 * half
+                        found = ((q, jnp.where(upper, 0.0, x)), (q + 1, jnp.where(upper, x, 0.0)))
+                    for q, x in found:
+                        hi, lo = split(x)
+                        cols = slice(side * ROWS, (side + 1) * ROWS)
+                        at = place(q, ROWS) + start
+                        bq[number, pl.ds(pl.multiple_of(at, 16), 16), cols] = hi
+                        at = at + GROUP * ROWS
+                        bq[number, pl.ds(pl.multiple_of(at, 16), 16), cols] = lo
             for j in range(3):
                 u, w = twice(geo[side, U0 + j, rows, :]), twice(geo[side, W0 + j, rows, :])
                 first = start + j * ROWS
-                put_rows(target, b * u, first, first + 6 * ROWS, slice(None))
+                put_rows(target, b * u, first, first + 6 * ROWS)
                 first += 3 * ROWS
-                put_rows(target, bd * u + b * w, first, first + 6 * ROWS, slice(None))
-
-    def add_to(ref, rows, value, i):
-        if i == 0:
-            ref[rows, :] = value
-        else:
-            ref[rows, :] += value
-
-    def gather_scalar(refs, cols):
-        both = mm(lb[:, cols], refs[0, cols, :])
-        rest = mm(lb[0 : 2 * ROWS, cols], refs[1, cols, :])
-        acc[0:ROWS, :] += both[ROWS : 2 * ROWS] + both[2 * ROWS : 3 * ROWS] + rest[ROWS:]
-        acc[ROWS : 2 * ROWS, :] += both[0:ROWS] + both[3 * ROWS :] + rest[0:ROWS]
+                put_rows(target, bd * u + b * w, first, first + 6 * ROWS)
+
+    def stream(left, i, rows, right, dims=NN):
+        start = 2 * GROUP * rows * i
+        full = pl.ds(pl.multiple_of(start, GROUP * rows), 2 * GROUP * rows)
+        high = pl.ds(pl.multiple_of(start, GROUP * rows), GROUP * rows)
+        both = mm(left[full, :], right[0], dims)
+        rest = mm(left[high, :], right[1], dims)
+        return both[0 : GROUP * rows] + both[GROUP * rows :] + rest
+
+    def weighted(target, value, i, rows, filters):
+        for k in range(GROUP):
+            target[...] += value[k * rows : (k + 1) * rows, :] * filters[pl.ds(GROUP * i + k, 1), 0:F]
 
     def gather_vector(m, near):
         cols = pl.ds(pl.multiple_of(m * TILE, TILE), TILE)
@@ -404,7 +424,7 @@
         accv[...] += both[0 : 6 * ROWS] + both[6 * ROWS :] + rest
 
     lax.fori_loop(0, ROWS // 8, functools.partial(geometry, side=0, table=c8[...]), 0)
-    build_pairs(0, lv0)
+    build_pairs(0, lv0, 0)
     pl.semaphore_wait(barrier, 8)
     coords = copies(csel, crecv, sendc, recvc, 1, True)
     first = copies(sel1, gemb, send1, recv1, 1, False)
@@ -414,14 +434,14 @@
     acc[...] = jnp.zeros((2 * ROWS, F), f32)
     accv[...] = jnp.zeros((6 * ROWS, F), f32)
 
-    def two_tiles(k, carry, base, last):
+    def two_tiles(k, carry, base, last, side):
         for half in range(2):
             m = base + 2 * k + half
             gather_vector(m, lv[half])
-            build_pairs(jnp.minimum(m + 1, last), lv[1 - half])
-        return carry
-
-    lax.fori_loop(0, PAIRS // 2, functools.partial(two_tiles, base=0, last=PAIRS - 1), 0)
+            build_pairs(jnp.minimum(m + 1, last), lv[1 - half], side)
+        return carry
+
+    lax.fori_loop(0, PAIRS // 2, functools.partial(two_tiles, base=0, last=PAIRS - 1, side=0), 0)
 
     for copy in coords + first:
         copy.wait()
@@ -429,21 +449,26 @@
     found = merged(crecv)
     twofold = found + pltpu.roll(found, GHOSTS, 1)
     lax.fori_loop(0, ROWS // 8, functools.partial(geometry, side=1, table=twofold), 0)
-    build_pairs(PAIRS, lv0)
-
-    spread_ghosts(pfs_s, lambda: phi[ROWS:TABLE, 0:F], f1, 0)
+    build_pairs(PAIRS, lv0, 1)
+
+    fill_ghosts(0, phi[ROWS:TABLE, 0:F])
     spread_ghosts(pfv_s, lambda: phi[ROWS:TABLE, F : 2 * F], f1, F)
     lax.fori_loop(
-        0, (TILES - PAIRS) // 2, functools.partial(two_tiles, base=PAIRS, last=TILES - 1), 0
+        0,
+        (TILES - PAIRS) // 2,
+        functools.partial(two_tiles, base=PAIRS, last=TILES - 1, side=1),
+        0,
     )
     gather_vector(TILES - 1, lv0)
 
 
-    def scalar_step(i, carry):
-        gather_scalar(pfs_s, pl.ds(pl.multiple_of(i * STEP, STEP), STEP))
-        return carry
-
-    lax.fori_loop(0, STEPS, scalar_step, 0)
+    def scalar_messages(i, carry):
+        for number in range(2):
+            value = stream(bq.at[number], i, ROWS, tab.at[0])
+            weighted(acc.at[number * ROWS : (number + 1) * ROWS, :], value, i, ROWS, f1)
+        return carry
+
+    lax.fori_loop(0, GROUPS, scalar_messages, 0)
     lr[...] = mm3(split(accv[...]), (wlr_s[0], wlr_s[1]))
 
     def part(j, side):
@@ -488,17 +513,11 @@
         def body(i, carry):
             start = pl.multiple_of(i * 16, 16)
             g = [pg[side, number, pl.ds(start, 16), :] for number in range(5)]
-            held = None
             for q, (a, s, c) in enumerate(own_waves(g[3], g[4])):
-                new = (g[0] * s, g[1] * s + g[2] * (a * c))
-                if q % 2 == 0:
-                    held = new
-                    continue
-                cols = slice((q - 1) * ROWS, (q + 1) * ROWS)
-                for value, first, second in ((1, 0, 3), (0, 1, 2)):
-                    hi, lo = split(jnp.concatenate([held[value], new[value]], 1))
-                    lt[pl.ds(start + side * ROWS + first * TABLE, 16), cols] = hi
-                    lt[pl.ds(start + side * ROWS + second * TABLE, 16), cols] = lo
+                hi, lo = split(jnp.concatenate([g[0] * s, g[1] * s + g[2] * (a * c)], 1))
+                at = start + place(q, TABLE) + side * ROWS
+                lt[pl.ds(pl.multiple_of(at, 16), 16), :] = hi
+                lt[pl.ds(pl.multiple_of(at + GROUP * TABLE, 16), 16), :] = lo
             return carry
 
         lax.fori_loop(0, count // 16, body, 0)
@@ -506,25 +525,24 @@
     turned(0, ROWS)
     turned(1, GHOSTS)
 
-    spread_own(p2_s, lambda: phi2[0, 0:ROWS, :], f2, 0)
-    spread_own(p2d_s, lambda: phi2[1, 0:ROWS, :], f2, 0)
+    fill_own(1, phi2[0, 0:ROWS, :])
+    fill_own(2, phi2[1, 0:ROWS, :])
 
     for copy in second:
         copy.wait()
     table_two(gnode[:, 0:F], gnode[:, F : 2 * F], ROWS, GHOSTS)
-    spread_ghosts(p2_s, lambda: phi2[0, ROWS:TABLE, :], f2, 0)
-    spread_ghosts(p2d_s, lambda: phi2[1, ROWS:TABLE, :], f2, 0)
+    fill_ghosts(1, phi2[0, ROWS:TABLE, :])
+    fill_ghosts(2, phi2[1, ROWS:TABLE, :])
     acc[...] = jnp.zeros((2 * ROWS, F), f32)
 
     def messages_two(i, carry):
-        cols = pl.ds(pl.multiple_of(i * STEP, STEP), STEP)
-        gather_scalar(p2_s, cols)
-        both = mm(lb[ROWS : 3 * ROWS, cols], p2d_s[0, cols, :])
-        rest = mm(lb[ROWS : 2 * ROWS, cols], p2d_s[1, cols, :])
-        acc[ROWS : 2 * ROWS, :] += both[0:ROWS] + both[ROWS:] + rest
-        return carry
-
-    lax.fori_loop(0, STEPS, messages_two, 0)
+        value = stream(bq.at[0], i, ROWS, tab.at[1])
+        weighted(acc.at[0:ROWS, :], value, i, ROWS, f2)
+        value = stream(bq.at[1], i, ROWS, tab.at[1]) + stream(bq.at[0], i, ROWS, tab.at[2])
+        weighted(acc.at[ROWS : 2 * ROWS, :], value, i, ROWS, f2)
+        return carry
+
+    lax.fori_loop(0, GROUPS, messages_two, 0)
     st = node[:, 0:F] + acc[0:ROWS, :]
     std = node[:, F : 2 * F] + acc[ROWS : 2 * ROWS, :]
 
@@ -539,43 +557,22 @@
         split(top * (sig * (1.0 - sig) * (2.0 + v * (1.0 - 2.0 * sig))) * vd), whs, NT
     )
 
-    muf = (muf0, muf1)
-
-    def scaled(i):
-        for q in range(4 * i, 4 * i + 4):
-            weights = f2[q : q + 1, :]
-            rows = slice(q % 4 * ROWS, (q % 4 + 1) * ROWS)
-            for number in range(2):
-                hi, lo = split(mu[number] * weights)
-                muf[i % 2][2 * number, rows, :] = hi
-                muf[i % 2][2 * number + 1, rows, :] = lo
-
-    def turned_messages(i):
-        cols = slice(i * 4 * ROWS, (i + 1) * 4 * ROWS)
-        right = muf[i % 2]
-        both = mm(lt[:, cols], right[0])
-        rest = mm(lt[0 : 2 * TABLE, cols], right[1])
-        also = mm(lt[TABLE : 3 * TABLE, cols], right[2])
-        more = mm(lt[TABLE : 2 * TABLE, cols], right[3])
-        add_to(
-            bar,
-            slice(0, TABLE),
-            both[TABLE : 2 * TABLE] + both[2 * TABLE : 3 * TABLE] + rest[TABLE:],
-            i,
-        )
-        add_to(
-            bar,
-            slice(TABLE, 2 * TABLE),
-            (both[0:TABLE] + both[3 * TABLE :] + rest[0:TABLE])
-            + (also[0:TABLE] + also[TABLE:] + more),
-            i,
-        )
-
-    for i in range(NR // 4 + 1):
-        if i < NR // 4:
-            scaled(i)
-        if i > 0:
-            turned_messages(i - 1)
+    for number in range(2):
+        hi, lo = split(mu[number])
+        for part_of, value in ((0, hi), (1, lo)):
+            wmu[part_of, 0:ROWS, number * F : (number + 1) * F] = value
+            if number == 0:
+                wmu[part_of, ROWS : 2 * ROWS, F : 2 * F] = value
+    wmu[:, ROWS : 2 * ROWS, 0:F] = jnp.zeros((2, ROWS, F), bf16)
+    bar[...] = jnp.zeros((2 * TABLE, F), f32)
+
+    def turned_messages(i, carry):
+        value = stream(lt, i, TABLE, wmu)
+        weighted(bar.at[0:TABLE, :], value[:, 0:F], i, TABLE, f2)
+        weighted(bar.at[TABLE : 2 * TABLE, :], value[:, F : 2 * F], i, TABLE, f2)
+        return carry
+
+    lax.fori_loop(0, GROUPS, turned_messages, 0)
     back = mm3(split(bar[...]), w2[1], NT)
     v, vd = pre2[0], pre2[1]
     sig = sigmoid(v)
@@ -590,25 +587,26 @@
     for copy in third:
         copy.start()
 
-    m = split(mu[0])
-    md = split(mu[1])
-    high = jnp.concatenate([m[0], md[0]], 0)
-    full = jnp.concatenate([high, m[1], md[1]], 0)
-    ours = jnp.concatenate(m, 0)
+    def scale_rows(q, carry, filters):
+        weights = filters[pl.ds(q, 1), 0:F]
+        for number in range(2):
+            hi, lo = split(mu[number] * weights)
+            at = place(q, ROWS)
+            scaled[number, pl.ds(pl.multiple_of(at, ROWS), ROWS), :] = hi
+            scaled[number, pl.ds(pl.multiple_of(at + GROUP * ROWS, ROWS), ROWS), :] = lo
+        return carry
+
+    lax.fori_loop(0, NR, functools.partial(scale_rows, filters=f2), 0)
 
     def pairs_two(i, carry):
-        cols = pl.ds(pl.multiple_of(i * STEP, STEP), STEP)
-        both = mm(full, p2_s[0, cols, :], NT)
-        rest = mm(high, p2_s[1, cols, :], NT)
-        also = mm(ours, p2d_s[0, cols, :], NT)
-        more = mm(m[0], p2d_s[1, cols, :], NT)
-        two[0:ROWS, cols] = both[0:ROWS] + both[2 * ROWS : 3 * ROWS] + rest[0:ROWS]
-        two[ROWS : 2 * ROWS, cols] = (
-            both[ROWS : 2 * ROWS] + both[3 * ROWS :] + rest[ROWS:]
-        ) + (also[0:ROWS] + also[ROWS:] + more)
-        return carry
-
-    lax.fori_loop(0, STEPS, pairs_two, 0)
+        rows = pl.ds(pl.multiple_of(i * GROUP * ROWS, ROWS), GROUP * ROWS)
+        two[0, rows, :] = stream(scaled.at[0], i, ROWS, tab.at[1], NT)
+        two[1, rows, :] = stream(scaled.at[1], i, ROWS, tab.at[1], NT) + stream(
+            scaled.at[0], i, ROWS, tab.at[2], NT
+        )
+        return carry
+
+    lax.fori_loop(0, GROUPS, pairs_two, 0)
 
     for copy in third:
         copy.wait()
@@ -631,32 +629,32 @@
     hi, lo = split(mm3(split(lr[...]), wlr, NT))
     vbar[0 : 6 * ROWS, :] = hi
     vbar[6 * ROWS :, :] = lo
-    for number in range(2):
-        hi, lo = split(mu[number])
-        nus[number * ROWS : (number + 1) * ROWS, :] = hi
-        nus[(2 + number) * ROWS : (3 + number) * ROWS, :] = lo
+    lax.fori_loop(0, NR, functools.partial(scale_rows, filters=f1), 0)
+
+    def pairs_scalar(i, carry):
+        rows = pl.ds(pl.multiple_of(i * GROUP * ROWS, ROWS), GROUP * ROWS)
+        for number in range(2):
+            two[number, rows, :] += stream(scaled.at[number], i, ROWS, tab.at[0], NT)
+        return carry
+
+    lax.fori_loop(0, GROUPS, pairs_scalar, 0)
     out = (out0, out1)
 
     def pairs_one(m, target):
         cols = pl.ds(pl.multiple_of(m * TILE, TILE), TILE)
-        both = mm(nus[...], pfs_s[0, cols, :], NT)
-        rest = mm(nus[0 : 2 * ROWS, :], pfs_s[1, cols, :], NT)
-        target[0 : 2 * ROWS, :] = two[:, cols] + (both[0 : 2 * ROWS] + both[2 * ROWS :] + rest)
         both = mm(vbar[...], pfv_s[0, cols, :], NT)
         rest = mm(vbar[0 : 6 * ROWS, :], pfv_s[1, cols, :], NT)
-        target[2 * ROWS :, :] = both[0 : 6 * ROWS] + both[6 * ROWS :] + rest
+        target[...] = both[0 : 6 * ROWS] + both[6 * ROWS :] + rest
 
     upper = lax.broadcasted_iota(jnp.int32, (8, ROWS), 1) >= GHOSTS
 
-    def sum_waves(m, source):
-        side = jnp.where(m < PAIRS, 0, 1)
-        base = jnp.where(m < PAIRS, 2 * m + 1, 4 * (m - PAIRS) + 1).astype(f32)
-        jump = jnp.where(m < PAIRS, 1.0, 2.0)
-        ghosts_on = jnp.where(m < PAIRS, 0.0, 1.0)
-        a = [
-            KAPPA * (base + half * jump + ghosts_on * jnp.where(upper, 1.0, 0.0))
-            for half in range(2)
-        ]
+    def sum_waves(m, source, side):
+        if side == 0:
+            first = [2 * m + half for half in range(2)]
+            a = [KAPPA * (q + 1).astype(f32) for q in first]
+        else:
+            first = [4 * (m - PAIRS) + 2 * half for half in range(2)]
+            a = [KAPPA * ((q + 1).astype(f32) + jnp.where(upper, 1.0, 0.0)) for q in first]
         aa = [x * x for x in a]
         for start in range(0, ROWS, 8):
             rows = slice(start, start + 8)
@@ -667,17 +665,26 @@
                 ac = waves[1, 2 * m + half, rows, :]
                 ss = s * aa[half]
                 cols = slice(half * ROWS, (half + 1) * ROWS)
-                y = [source[start + k * ROWS : start + k * ROWS + 8, cols] for k in range(8)]
-                along = y[0] + u[0] * y[2] + u[1] * y[3] + u[2] * y[4]
-                along_d = y[1] + u[0] * y[5] + u[1] * y[6] + u[2] * y[7]
+                y = [source[start + k * ROWS : start + k * ROWS + 8, cols] for k in range(6)]
+                own = slice(side * ROWS, (side + 1) * ROWS)
+                near = []
+                for number in range(2):
+                    at = pl.multiple_of(first[half] * ROWS + start, 8)
+                    value = two[number, pl.ds(at, 8), own]
+                    if side == 1:
+                        at = pl.multiple_of(at + ROWS, 8)
+                        value = jnp.where(upper, two[number, pl.ds(at, 8), own], value)
+                    near.append(value)
+                along = near[0] + u[0] * y[0] + u[1] * y[1] + u[2] * y[2]
+                along_d = near[1] + u[0] * y[3] + u[1] * y[4] + u[2] * y[5]
                 for j in range(3):
-                    total[j] += s * y[2 + j]
-                    total[3 + j] += ac * y[2 + j]
-                    total[6 + j] += s * y[5 + j]
-                total[9] += s * y[0]
-                total[10] += ac * y[0]
+                    total[j] += s * y[j]
+                    total[3 + j] += ac * y[j]
+                    total[6 + j] += s * y[3 + j]
+                total[9] += s * near[0]
+                total[10] += ac * near[0]
                 total[11] += ss * along
-                total[12] += s * y[1]
+                total[12] += s * near[1]
                 total[13] += ac * along_d
             for number in range(14):
                 sums[side, number, rows, :] = total[number]
@@ -685,22 +692,22 @@
     sums[...] = jnp.zeros(sums.shape, f32)
     pairs_one(PAIRS, out0)
 
-    def two_sums(k, carry, first, second, base, last):
+    def two_sums(k, carry, first, second, base, last, side):
         for half in range(2):
             ahead, behind = (first, second) if half == 0 else (second, first)
             m = base + 2 * k + half
             pairs_one(jnp.minimum(m + 1, last), ahead)
-            sum_waves(m, behind)
+            sum_waves(m, behind, side)
         return carry
 
     lax.fori_loop(
         0,
         (TILES - PAIRS) // 2,
-        functools.partial(two_sums, first=out1, second=out0, base=PAIRS, last=TILES - 1),
+        functools.partial(two_sums, first=out1, second=out0, base=PAIRS, last=TILES - 1, side=1),
         0,
     )
     pairs_one(0, out1)
-    sum_waves(TILES - 1, out0)
+    sum_waves(jnp.int32(TILES - 1), out0, 1)
 
     def offsets_back(i, carry, side):
         rows = pl.ds(pl.multiple_of(i * 8, 8), 8)
@@ -752,7 +759,7 @@
     lax.fori_loop(
         0,
         PAIRS // 2,
-        functools.partial(two_sums, first=out0, second=out1, base=0, last=PAIRS - 1),
+        functools.partial(two_sums, first=out0, second=out1, base=0, last=PAIRS - 1, side=0),
         0,
     )
     lax.fori_loop(0, ROWS // 8, functools.partial(offsets_back, side=0), 0)
@@ -814,16 +821,14 @@
         v32(6, ROWS, ROWS),
         v32(2, 13, ROWS, ROWS),
         v32(2, NR + PAIRS, ROWS, ROWS),
-        v16(4 * ROWS, WIDE),
+        v16(2, 2 * NR * ROWS, TILE),
         v16(12 * ROWS, TILE),
         v16(12 * ROWS, TILE),
-        v16(4 * TABLE, NR * ROWS),
+        v16(2 * NR * TABLE, 2 * ROWS),
         v16(2, WIDE, F),
-        v16(2, WIDE, F),
-        v16(2, WIDE, F),
-        v16(2, WIDE, F),
-        v16(4, 4 * ROWS, F),
-        v16(4, 4 * ROWS, F),
+        v16(3, 2, 2 * ROWS, F),
+        v16(2, 2 * ROWS, 2 * F),
+        v16(2, 2 * NR * ROWS, F),
         v32(TABLE, 2 * F),
         v32(2 * ROWS, F),
         v32(6 * ROWS, F),
@@ -833,13 +838,12 @@
         v32(2, TABLE, F),
         v32(2, ROWS, F),
         v32(2 * TABLE, F),
-        v32(8 * ROWS, TILE),
-        v32(8 * ROWS, TILE),
+        v32(6 * ROWS, TILE),
+        v32(6 * ROWS, TILE),
         v32(3 * F, 3 * F),
-        v32(2 * ROWS, WIDE),
+        v32(2, NR * ROWS, TILE),
         v32(2, 14, ROWS, ROWS),
         v16(12 * ROWS, F),
-        v16(4 * ROWS, F),
         v32(2, 6, ROWS, ROWS),
     ] + [dma] * 10 + [pltpu.SemaphoreType.DMA((15,))]
     out = jax.ShapeDtypeStruct((3, ROWS), f32)

time: 60.7 us -> 62.6 us (1.031)
  Pallas kernels: 57.3 us -> 59.2 us
    pallas_call x1, Pallas kernels: 57.3 us -> 59.2 us  [per_device(): pl.pallas_call(functools.partial(kernel, nx, ny), out_shape=(out, out), i...]
where the time goes in v4:
time: 62.6 us; the launch traced here: 62.4 us
  Pallas kernels  59.2 us (95%)
  local copies, waits for them, and re-layouts  1.89 us (3%)
  between operations  1.3 us (2%)
    pallas_call x1, Pallas kernels, per_device(): pl.pallas_call(functools.partial(kernel, nx, ny), out_shape=(out, out), i...  59.2 us
    unnamed x6, local copies, waits for them, and re-layouts  1.89 us

profile of v4, /device:TPU:0, one launch (start us, length us, event | category | flops | bytes accessed | tf_op | source)
XLA Modules:
  0.0 62.4 jit_solution(4355339060538028005)
XLA Ops:
  1.3 59.2 %shard_map.167 = (f32[3,128]{1,0:T(4,128)}, f32[3,128]{1,0:T(4,128)}) custom-call(f32[3,128]{1,0:T(4,128)} %pos_in.1, f32[3,128]{1,0:T(4,128)} %tan_in.1, f32[128,256]{1,0:T(8,128)} %emb_in.1, s32[1]{0:T(128)S(6)} %copy.20.cnt, s32[32,128]{1,0:T(8,128)} %nbr_in.1, s32[1,64]{1,0:T(1,128)} %snd_in.1, f32[256,256]{1,0:T(8,128)} %w1i.1, f32[256,512]{1,0:T(8,128)} %w1o.1, ...), custom_call_target="tpu_custom_call" | custom-call | tf_op jit(solution)/shard_map/pallas_call | solution.py:850
  60.5 0.0 copy-start.1
  60.5 0.7 %copy-done.1 = f32[3,128]{1,0:T(4,128)S(1)} copy-done((f32[3,128]{1,0:T(4,128)S(1)}, f32[3,128]{1,0:T(4,128)}, u32[]{:S(2)}) %copy-start.1) | copy-done | bytes 1560
  61.2 0.0 copy-start
  61.2 0.6 copy.21
  61.7 0.1 copy-done
  61.8 0.6 copy.22
Async XLA Ops:
  60.5 0.7 %copy-start.1 = (f32[3,128]{1,0:T(4,128)S(1)}, f32[3,128]{1,0:T(4,128)}, u32[]{:S(2)}) copy-start(f32[3,128]{1,0:T(4,128)} %get-tuple-element.4) | copy-start | bytes 4612
  61.2 0.7 %copy-start = (f32[3,128]{1,0:T(4,128)S(1)}, f32[3,128]{1,0:T(4,128)}, u32[]{:S(2)}) copy-start(f32[3,128]{1,0:T(4,128)} %get-tuple-element.5) | copy-start | bytes 4612

commit v5 on v3

--- a/solution.py
+++ b/solution.py
@@ -25,8 +25,9 @@
 TILE = 256
 TILES = NR * TABLE // TILE
 WIDE = TILES * TILE
-STEP = 3 * TILE
+STEP = 5 * TILE
 STEPS = WIDE // STEP
+OWN_STEPS = 2
 
 
 def split(x):
@@ -166,8 +167,7 @@
     pfv_s,
     p2_s,
     p2d_s,
-    muf0,
-    muf1,
+    muf,
     phi,
     acc,
     accv,
@@ -497,8 +497,9 @@
                 cols = slice((q - 1) * ROWS, (q + 1) * ROWS)
                 for value, first, second in ((1, 0, 3), (0, 1, 2)):
                     hi, lo = split(jnp.concatenate([held[value], new[value]], 1))
-                    lt[pl.ds(start + side * ROWS + first * TABLE, 16), cols] = hi
-                    lt[pl.ds(start + side * ROWS + second * TABLE, 16), cols] = lo
+                    at = 4 * side * ROWS
+                    lt[pl.ds(start + at + first * count, 16), cols] = hi
+                    lt[pl.ds(start + at + second * count, 16), cols] = lo
             return carry
 
         lax.fori_loop(0, count // 16, body, 0)
@@ -508,12 +509,6 @@
 
     spread_own(p2_s, lambda: phi2[0, 0:ROWS, :], f2, 0)
     spread_own(p2d_s, lambda: phi2[1, 0:ROWS, :], f2, 0)
-
-    for copy in second:
-        copy.wait()
-    table_two(gnode[:, 0:F], gnode[:, F : 2 * F], ROWS, GHOSTS)
-    spread_ghosts(p2_s, lambda: phi2[0, ROWS:TABLE, :], f2, 0)
-    spread_ghosts(p2d_s, lambda: phi2[1, ROWS:TABLE, :], f2, 0)
     acc[...] = jnp.zeros((2 * ROWS, F), f32)
 
     def messages_two(i, carry):
@@ -524,7 +519,14 @@
         acc[ROWS : 2 * ROWS, :] += both[0:ROWS] + both[ROWS:] + rest
         return carry
 
-    lax.fori_loop(0, STEPS, messages_two, 0)
+    lax.fori_loop(0, OWN_STEPS, messages_two, 0)
+
+    for copy in second:
+        copy.wait()
+    table_two(gnode[:, 0:F], gnode[:, F : 2 * F], ROWS, GHOSTS)
+    spread_ghosts(p2_s, lambda: phi2[0, ROWS:TABLE, :], f2, 0)
+    spread_ghosts(p2d_s, lambda: phi2[1, ROWS:TABLE, :], f2, 0)
+    messages_two(OWN_STEPS, 0)
     st = node[:, 0:F] + acc[0:ROWS, :]
     std = node[:, F : 2 * F] + acc[ROWS : 2 * ROWS, :]
 
@@ -539,57 +541,65 @@
         split(top * (sig * (1.0 - sig) * (2.0 + v * (1.0 - 2.0 * sig))) * vd), whs, NT
     )
 
-    muf = (muf0, muf1)
-
     def scaled(i):
         for q in range(4 * i, 4 * i + 4):
             weights = f2[q : q + 1, :]
             rows = slice(q % 4 * ROWS, (q % 4 + 1) * ROWS)
             for number in range(2):
                 hi, lo = split(mu[number] * weights)
-                muf[i % 2][2 * number, rows, :] = hi
-                muf[i % 2][2 * number + 1, rows, :] = lo
-
-    def turned_messages(i):
+                muf[i, 2 * number, rows, :] = hi
+                muf[i, 2 * number + 1, rows, :] = lo
+
+    def turned_messages(i, at, count):
         cols = slice(i * 4 * ROWS, (i + 1) * 4 * ROWS)
-        right = muf[i % 2]
-        both = mm(lt[:, cols], right[0])
-        rest = mm(lt[0 : 2 * TABLE, cols], right[1])
-        also = mm(lt[TABLE : 3 * TABLE, cols], right[2])
-        more = mm(lt[TABLE : 2 * TABLE, cols], right[3])
+        top = 4 * at
+        both = mm(lt[top : top + 4 * count, cols], muf[i, 0])
+        rest = mm(lt[top : top + 2 * count, cols], muf[i, 1])
+        also = mm(lt[top + count : top + 3 * count, cols], muf[i, 2])
+        more = mm(lt[top + count : top + 2 * count, cols], muf[i, 3])
         add_to(
             bar,
-            slice(0, TABLE),
-            both[TABLE : 2 * TABLE] + both[2 * TABLE : 3 * TABLE] + rest[TABLE:],
+            slice(at, at + count),
+            both[count : 2 * count] + both[2 * count : 3 * count] + rest[count:],
             i,
         )
         add_to(
             bar,
-            slice(TABLE, 2 * TABLE),
-            (both[0:TABLE] + both[3 * TABLE :] + rest[0:TABLE])
-            + (also[0:TABLE] + also[TABLE:] + more),
+            slice(TABLE + at, TABLE + at + count),
+            (both[0:count] + both[3 * count :] + rest[0:count])
+            + (also[0:count] + also[count:] + more),
             i,
         )
+
+    def back_to_states(at, count):
+        near, far = slice(at, at + count), slice(TABLE + at, TABLE + at + count)
+        v, vd = pre2[0, near, :], pre2[1, near, :]
+        sig = sigmoid(v)
+        slope = sig * (1.0 + v * (1.0 - sig))
+        curve = sig * (1.0 - sig) * (2.0 + v * (1.0 - 2.0 * sig))
+        both = mm3(split(jnp.concatenate([bar[near, :], bar[far, :]], 0)), w2[1], NT)
+        first, second = both[0:count], both[count:]
+        both = jnp.concatenate([first * slope, second * slope + first * curve * vd], 0)
+        both = mm3(split(both), w2[0], NT)
+        bar[near, :] = both[0:count]
+        bar[far, :] = both[count:]
 
     for i in range(NR // 4 + 1):
         if i < NR // 4:
             scaled(i)
         if i > 0:
-            turned_messages(i - 1)
-    back = mm3(split(bar[...]), w2[1], NT)
-    v, vd = pre2[0], pre2[1]
-    sig = sigmoid(v)
-    slope = sig * (1.0 + v * (1.0 - sig))
-    curve = sig * (1.0 - sig) * (2.0 + v * (1.0 - 2.0 * sig))
-    bar[0:TABLE, :] = back[0:TABLE] * slope
-    bar[TABLE : 2 * TABLE, :] = back[TABLE : 2 * TABLE] * slope + back[0:TABLE] * curve * vd
-    bar[...] = mm3(split(bar[...]), w2[0], NT)
+            turned_messages(i - 1, ROWS, GHOSTS)
+    back_to_states(ROWS, GHOSTS)
     src3[:, 0:F] = bar[ROWS:TABLE, :]
     src3[:, F : 2 * F] = bar[TABLE + ROWS : 2 * TABLE, :]
     third = copies(src3, rnode, send3, recv3, -1, False)
     for copy in third:
         copy.start()
 
+    for i in range(NR // 4):
+        turned_messages(i, 0, ROWS)
+    back_to_states(0, ROWS)
+
     m = split(mu[0])
     md = split(mu[1])
     high = jnp.concatenate([m[0], md[0]], 0)
@@ -597,7 +607,7 @@
     ours = jnp.concatenate(m, 0)
 
     def pairs_two(i, carry):
-        cols = pl.ds(pl.multiple_of(i * STEP, STEP), STEP)
+        cols = pl.ds(pl.multiple_of(i * 3 * TILE, 3 * TILE), 3 * TILE)
         both = mm(full, p2_s[0, cols, :], NT)
         rest = mm(high, p2_s[1, cols, :], NT)
         also = mm(ours, p2d_s[0, cols, :], NT)
@@ -608,7 +618,7 @@
         ) + (also[0:ROWS] + also[ROWS:] + more)
         return carry
 
-    lax.fori_loop(0, STEPS, pairs_two, 0)
+    lax.fori_loop(0, TILES // 3, pairs_two, 0)
 
     for copy in third:
         copy.wait()
@@ -822,8 +832,7 @@
         v16(2, WIDE, F),
         v16(2, WIDE, F),
         v16(2, WIDE, F),
-        v16(4, 4 * ROWS, F),
-        v16(4, 4 * ROWS, F),
+        v16(NR // 4, 4, 4 * ROWS, F),
         v32(TABLE, 2 * F),
         v32(2 * ROWS, F),
         v32(6 * ROWS, F),

time: 60.7 us -> 58.5 us (0.964)
  Pallas kernels: 57.3 us -> 55.1 us
    pallas_call x1, Pallas kernels: 57.3 us -> 55.1 us  [per_device(): pl.pallas_call(functools.partial(kernel, nx, ny), out_shape=(out, out), i...]
where the time goes in v5:
time: 58.5 us; the launch traced here: 58.3 us
  Pallas kernels  55.1 us (94%)
  local copies, waits for them, and re-layouts  1.89 us (3%)
  between operations  1.3 us (2%)
    pallas_call x1, Pallas kernels, per_device(): pl.pallas_call(functools.partial(kernel, nx, ny), out_shape=(out, out), i...  55.1 us
    unnamed x6, local copies, waits for them, and re-layouts  1.89 us

profile of v5, /device:TPU:0, one launch (start us, length us, event | category | flops | bytes accessed | tf_op | source)
XLA Modules:
  0.0 58.3 jit_solution(11776398055784737573)
XLA Ops:
  1.3 55.1 %shard_map.167 = (f32[3,128]{1,0:T(4,128)}, f32[3,128]{1,0:T(4,128)}) custom-call(f32[3,128]{1,0:T(4,128)} %pos_in.1, f32[3,128]{1,0:T(4,128)} %tan_in.1, f32[128,256]{1,0:T(8,128)} %emb_in.1, s32[1]{0:T(128)S(6)} %copy.20.cnt, s32[32,128]{1,0:T(8,128)} %nbr_in.1, s32[1,64]{1,0:T(1,128)} %snd_in.1, f32[256,256]{1,0:T(8,128)} %w1i.1, f32[256,512]{1,0:T(8,128)} %w1o.1, ...), custom_call_target="tpu_custom_call" | custom-call | tf_op jit(solution)/shard_map/pallas_call | solution.py:855
  56.4 0.0 copy-start.1
  56.4 0.7 %copy-done.1 = f32[3,128]{1,0:T(4,128)S(1)} copy-done((f32[3,128]{1,0:T(4,128)S(1)}, f32[3,128]{1,0:T(4,128)}, u32[]{:S(2)}) %copy-start.1) | copy-done | bytes 1560
  57.0 0.0 copy-start
  57.0 0.6 copy.21
  57.6 0.1 copy-done
  57.7 0.6 copy.22
Async XLA Ops:
  56.4 0.7 %copy-start.1 = (f32[3,128]{1,0:T(4,128)S(1)}, f32[3,128]{1,0:T(4,128)}, u32[]{:S(2)}) copy-start(f32[3,128]{1,0:T(4,128)} %get-tuple-element.4) | copy-start | bytes 4612
  57.0 0.7 %copy-start = (f32[3,128]{1,0:T(4,128)S(1)}, f32[3,128]{1,0:T(4,128)}, u32[]{:S(2)}) copy-start(f32[3,128]{1,0:T(4,128)} %get-tuple-element.5) | copy-start | bytes 4612

commit v6 on v5

--- a/solution.py
+++ b/solution.py
@@ -647,18 +647,22 @@
         nus[(2 + number) * ROWS : (3 + number) * ROWS, :] = lo
     out = (out0, out1)
 
-    def pairs_one(m, target):
-        cols = pl.ds(pl.multiple_of(m * TILE, TILE), TILE)
+    def pairs_one(m, target, count):
+        width = count * TILE
+        cols = pl.ds(pl.multiple_of(m * TILE, TILE), width)
         both = mm(nus[...], pfs_s[0, cols, :], NT)
         rest = mm(nus[0 : 2 * ROWS, :], pfs_s[1, cols, :], NT)
-        target[0 : 2 * ROWS, :] = two[:, cols] + (both[0 : 2 * ROWS] + both[2 * ROWS :] + rest)
+        target[0 : 2 * ROWS, 0:width] = two[:, cols] + (
+            both[0 : 2 * ROWS] + both[2 * ROWS :] + rest
+        )
         both = mm(vbar[...], pfv_s[0, cols, :], NT)
         rest = mm(vbar[0 : 6 * ROWS, :], pfv_s[1, cols, :], NT)
-        target[2 * ROWS :, :] = both[0 : 6 * ROWS] + both[6 * ROWS :] + rest
+        target[2 * ROWS :, 0:width] = both[0 : 6 * ROWS] + both[6 * ROWS :] + rest
 
     upper = lax.broadcasted_iota(jnp.int32, (8, ROWS), 1) >= GHOSTS
 
-    def sum_waves(m, source):
+    def sum_waves(m, source, place):
+        m = jnp.int32(m)
         side = jnp.where(m < PAIRS, 0, 1)
         base = jnp.where(m < PAIRS, 2 * m + 1, 4 * (m - PAIRS) + 1).astype(f32)
         jump = jnp.where(m < PAIRS, 1.0, 2.0)
@@ -676,7 +680,7 @@
                 s = waves[0, 2 * m + half, rows, :]
                 ac = waves[1, 2 * m + half, rows, :]
                 ss = s * aa[half]
-                cols = slice(half * ROWS, (half + 1) * ROWS)
+                cols = slice(place * TILE + half * ROWS, place * TILE + (half + 1) * ROWS)
                 y = [source[start + k * ROWS : start + k * ROWS + 8, cols] for k in range(8)]
                 along = y[0] + u[0] * y[2] + u[1] * y[3] + u[2] * y[4]
                 along_d = y[1] + u[0] * y[5] + u[1] * y[6] + u[2] * y[7]
@@ -693,24 +697,17 @@
                 sums[side, number, rows, :] = total[number]
 
     sums[...] = jnp.zeros(sums.shape, f32)
-    pairs_one(PAIRS, out0)
-
-    def two_sums(k, carry, first, second, base, last):
-        for half in range(2):
-            ahead, behind = (first, second) if half == 0 else (second, first)
-            m = base + 2 * k + half
-            pairs_one(jnp.minimum(m + 1, last), ahead)
-            sum_waves(m, behind)
-        return carry
-
-    lax.fori_loop(
-        0,
-        (TILES - PAIRS) // 2,
-        functools.partial(two_sums, first=out1, second=out0, base=PAIRS, last=TILES - 1),
-        0,
-    )
-    pairs_one(0, out1)
-    sum_waves(TILES - 1, out0)
+    def sum_both(m, source):
+        sum_waves(m, source, 0)
+        sum_waves(m + 1, source, 1)
+
+    pairs_one(PAIRS, out0, 2)
+    pairs_one(PAIRS + 2, out1, 2)
+    sum_both(PAIRS, out0)
+    pairs_one(PAIRS + 4, out0, 1)
+    sum_both(PAIRS + 2, out1)
+    pairs_one(0, out1, 2)
+    sum_waves(PAIRS + 4, out0, 0)
 
     def offsets_back(i, carry, side):
         rows = pl.ds(pl.multiple_of(i * 8, 8), 8)
@@ -759,12 +756,15 @@
     for copy in last:
         copy.start()
 
-    lax.fori_loop(
-        0,
-        PAIRS // 2,
-        functools.partial(two_sums, first=out0, second=out1, base=0, last=PAIRS - 1),
-        0,
-    )
+    def two_sums(k, carry):
+        pairs_one(4 * k + 2, out0, 2)
+        sum_both(4 * k, out1)
+        pairs_one(4 * k + 4, out1, 2)
+        sum_both(4 * k + 2, out0)
+        return carry
+
+    lax.fori_loop(0, 2, two_sums, 0)
+    sum_both(8, out1)
     lax.fori_loop(0, ROWS // 8, functools.partial(offsets_back, side=0), 0)
     for j in range(6):
         own = pg[0, j]
@@ -842,8 +842,8 @@
         v32(2, TABLE, F),
         v32(2, ROWS, F),
         v32(2 * TABLE, F),
-        v32(8 * ROWS, TILE),
-        v32(8 * ROWS, TILE),
+        v32(8 * ROWS, 2 * TILE),
+        v32(8 * ROWS, 2 * TILE),
         v32(3 * F, 3 * F),
         v32(2 * ROWS, WIDE),
         v32(2, 14, ROWS, ROWS),

time: 58.5 us -> 57.7 us (0.986)
  Pallas kernels: 55.1 us -> 54.3 us
    pallas_call x1, Pallas kernels: 55.1 us -> 54.3 us  [per_device(): pl.pallas_call(functools.partial(kernel, nx, ny), out_shape=(out, out), i...]
where the time goes in v6:
time: 57.7 us; the launch traced here: 57.5 us
  Pallas kernels  54.3 us (94%)
  local copies, waits for them, and re-layouts  1.89 us (3%)
  between operations  1.3 us (2%)
    pallas_call x1, Pallas kernels, per_device(): pl.pallas_call(functools.partial(kernel, nx, ny), out_shape=(out, out), i...  54.3 us
    unnamed x6, local copies, waits for them, and re-layouts  1.89 us

profile of v6, /device:TPU:0, one launch (start us, length us, event | category | flops | bytes accessed | tf_op | source)
XLA Modules:
  0.0 57.5 jit_solution(12234966436506635309)
XLA Ops:
  1.3 54.3 %shard_map.167 = (f32[3,128]{1,0:T(4,128)}, f32[3,128]{1,0:T(4,128)}) custom-call(f32[3,128]{1,0:T(4,128)} %pos_in.1, f32[3,128]{1,0:T(4,128)} %tan_in.1, f32[128,256]{1,0:T(8,128)} %emb_in.1, s32[1]{0:T(128)S(6)} %copy.20.cnt, s32[32,128]{1,0:T(8,128)} %nbr_in.1, s32[1,64]{1,0:T(1,128)} %snd_in.1, f32[256,256]{1,0:T(8,128)} %w1i.1, f32[256,512]{1,0:T(8,128)} %w1o.1, ...), custom_call_target="tpu_custom_call" | custom-call | tf_op jit(solution)/shard_map/pallas_call | solution.py:855
  55.6 0.0 copy-start.1
  55.6 0.7 %copy-done.1 = f32[3,128]{1,0:T(4,128)S(1)} copy-done((f32[3,128]{1,0:T(4,128)S(1)}, f32[3,128]{1,0:T(4,128)}, u32[]{:S(2)}) %copy-start.1) | copy-done | bytes 1560
  56.3 0.0 copy-start
  56.3 0.6 %copy.21 = f32[3,128]{1,0:T(4,128)} copy(f32[3,128]{1,0:T(4,128)S(1)} %copy-done.1) | data formatting | bytes 3072
  56.9 0.1 copy-done
  56.9 0.6 %copy.22 = f32[3,128]{1,0:T(4,128)} copy(f32[3,128]{1,0:T(4,128)S(1)} %copy-done) | data formatting | bytes 3072
Async XLA Ops:
  55.6 0.7 %copy-start.1 = (f32[3,128]{1,0:T(4,128)S(1)}, f32[3,128]{1,0:T(4,128)}, u32[]{:S(2)}) copy-start(f32[3,128]{1,0:T(4,128)} %get-tuple-element.4) | copy-start | bytes 4612
  56.3 0.7 %copy-start = (f32[3,128]{1,0:T(4,128)S(1)}, f32[3,128]{1,0:T(4,128)}, u32[]{:S(2)}) copy-start(f32[3,128]{1,0:T(4,128)} %get-tuple-element.5) | copy-start | bytes 4612

commit v7 on v6

--- a/solution.py
+++ b/solution.py
@@ -126,8 +126,7 @@
     f2_in,
     wh,
     we_in,
-    force,
-    hess,
+    result,
     pos,
     tan,
     emb,
@@ -607,7 +606,7 @@
     ours = jnp.concatenate(m, 0)
 
     def pairs_two(i, carry):
-        cols = pl.ds(pl.multiple_of(i * 3 * TILE, 3 * TILE), 3 * TILE)
+        cols = pl.ds(pl.multiple_of(i * STEP, TILE), STEP)
         both = mm(full, p2_s[0, cols, :], NT)
         rest = mm(high, p2_s[1, cols, :], NT)
         also = mm(ours, p2d_s[0, cols, :], NT)
@@ -618,7 +617,7 @@
         ) + (also[0:ROWS] + also[ROWS:] + more)
         return carry
 
-    lax.fori_loop(0, TILES // 3, pairs_two, 0)
+    lax.fori_loop(0, STEPS, pairs_two, 0)
 
     for copy in third:
         copy.wait()
@@ -774,8 +773,7 @@
     hi, mid, lo = split3(merged(rpos))
     slots = onehot[1].astype(bf16)
     total = c8[...] + (mm(hi, slots) + (mm(mid, slots) + mm(lo, slots)))
-    force[...] = -total[0:3, :]
-    hess[...] = -total[3:6, :]
+    result[...] = -total
 
 
 def per_device(nx, ny, *arrays):
@@ -851,17 +849,17 @@
         v16(4 * ROWS, F),
         v32(2, 6, ROWS, ROWS),
     ] + [dma] * 10 + [pltpu.SemaphoreType.DMA((15,))]
-    out = jax.ShapeDtypeStruct((3, ROWS), f32)
-    return pl.pallas_call(
+    result = pl.pallas_call(
         functools.partial(kernel, nx, ny),
-        out_shape=(out, out),
+        out_shape=jax.ShapeDtypeStruct((8, ROWS), f32),
         in_specs=in_specs,
-        out_specs=(vmem, vmem),
+        out_specs=vmem,
         scratch_shapes=scratch,
         compiler_params=pltpu.CompilerParams(
             collective_id=0, has_side_effects=True, vmem_limit_bytes=67043328
         ),
     )(*arrays)
+    return result[0:3], result[3:6]
 
 
 def solution(mesh):

time: 57.7 us -> 56.8 us (0.984)
    unnamed x6 -> x0, local copies, waits for them, and re-layouts: 1.89 us -> none
    slice x0 -> x1, local copies, waits for them, and re-layouts: none -> 1.33 us  [per_device(): return (result[0:3], result[3:6])]
where the time goes in v7:
time: 56.8 us; the launch traced here: 56.6 us
  Pallas kernels  54 us (95%)
  local copies, waits for them, and re-layouts  1.33 us (2%)
  between operations  1.29 us (2%)
    pallas_call x1, Pallas kernels, per_device(): pl.pallas_call(functools.partial(kernel, nx, ny), out_shape=jax.ShapeDtyp...  54 us
    slice x1, local copies, waits for them, and re-layouts, per_device(): return (result[0:3], result[3:6])  1.33 us

profile of v7, /device:TPU:0, one launch (start us, length us, event | category | flops | bytes accessed | tf_op | source)
XLA Modules:
  0.0 56.6 jit_solution(17089873889461923025)
XLA Ops:
  1.3 54.0 %shard_map.167 = f32[8,128]{1,0:T(8,128)} custom-call(f32[3,128]{1,0:T(4,128)} %pos_in.1, f32[3,128]{1,0:T(4,128)} %tan_in.1, f32[128,256]{1,0:T(8,128)} %emb_in.1, s32[1]{0:T(128)S(6)} %copy.18.cnt, s32[32,128]{1,0:T(8,128)} %nbr_in.1, s32[1,64]{1,0:T(1,128)} %snd_in.1, f32[256,256]{1,0:T(8,128)} %w1i.1, f32[256,512]{1,0:T(8,128)} %w1o.1, f32[20,512]{1,0:T(8,128)} %f1_in.1, ...), custom_call_target="tpu_custom_call" | custom-call | tf_op jit(solution)/shard_map/pallas_call | solution.py:852
  55.3 1.3 %fusion = (f32[3,128]{1,0:T(4,128)}, f32[3,128]{1,0:T(4,128)}) fusion(f32[8,128]{1,0:T(8,128)} %shard_map.167), kind=kLoop, calls=%fused_computation | loop fusion | bytes 6144 | tf_op jit(solution)/shard_map/slice | solution.py:862
